TPU v7x, 512 devices: a whole 4x8x8 slice. The times are simulated.
512 devices in a mesh: sec: 8 (over z_lo, x), gx: 16 (over y, core), gy: 4 (over z_hi).
Axes of the slice: x: 4, y: 8, z: 8 (z_hi: 4, z_lo: 2; z = z_hi * 2 + z_lo), core: 2. Of those that a mesh axis runs over, the one named last changes fastest.
Arguments:
- fields: float32 [8, 5, 512, 1024], P('sec', None, 'gx', 'gy'), may hold values from -1.5 to 6, as said below
- stored_rates: bfloat16 [8, 3, 5, 512, 1024], P('sec', None, None, 'gx', 'gy'), may hold values from -6 to 6
Outputs:
- advanced: float32 [8, 5, 512, 1024], P('sec', None, 'gx', 'gy')
Inputs may be any that keep to these rules, and one draw needn't show every extreme that they name: `fields`: for every level and cell: density in [0.6, 1.4], every velocity component within 0.9 in magnitude, pressure in [0.6, 1.4]; momenta are density times velocity and energy is pressure / 0.4 plus density times kinetic energy.
All inputs are finite; a program needn't handle non-finite values.
Results may differ from a plain program's by a relative error of at most 0.0005.
Values may be sent and summed in bfloat16 or wider, within the bound.
A program may use at most 64 MiB of HBM per device.

v0:
```python
import jax
import jax.numpy as jnp
from jax import lax
from jax.sharding import PartitionSpec as P

NZ = 32
TICKS = 3


TIME_STEP = 0.04
DYNAMIC_FRICTION = 0.4
CONDUCTIVITY = 0.5
GAMMA_LESS = 0.4
QUAD_WEIGHTS = (1.0 / 24.0, -5.0 / 24.0, 19.0 / 24.0, 9.0 / 24.0)


def with_halo(block, sides, width):
    for axis, dim in sides:
        count = lax.axis_size(axis)
        forward = [(i, i + 1) for i in range(count - 1)]
        forward.append((count - 1, 0))
        backward = [(target, source) for source, target in forward]
        low = lax.ppermute(
            lax.slice_in_dim(block, block.shape[dim] - width, None, axis=dim), axis, forward
        )
        high = lax.ppermute(lax.slice_in_dim(block, 0, width, axis=dim), axis, backward)
        block = jnp.concatenate([low, block, high], axis=dim)
    return block


def shifted(block, axis, distance):
    devices = range(lax.axis_size(axis))
    route = [(i - distance, i) for i in devices if i - distance in devices]
    return lax.ppermute(block, axis, route)


def shift_z(values, step, depth):
    column = lax.broadcasted_iota(jnp.int32, values.shape, values.ndim - 1) % depth
    unwrapped = jnp.roll(values, -step, axis=-1)
    if step > 0:
        wrapped = jnp.roll(values, depth - step, axis=-1)
        inside = column + step < depth
    else:
        wrapped = jnp.roll(values, -step - depth, axis=-1)
        inside = column + step >= 0
    return jnp.where(inside, unwrapped, wrapped)


def rates(matter_per_volume, mom_x, mom_y, mom_z, energy, window, depth):
    vel_x = mom_x / matter_per_volume
    vel_y = mom_y / matter_per_volume
    vel_z = mom_z / matter_per_volume
    motion_half_square = 0.5 * (vel_x * vel_x + vel_y * vel_y + vel_z * vel_z)
    normal_stress_scalar = GAMMA_LESS * (energy - matter_per_volume * motion_half_square)
    gas_warmth_field = normal_stress_scalar / matter_per_volume
    enthalpy = energy + normal_stress_scalar

    def diff_x(values):
        return (window(values, 1, 0) - window(values, -1, 0)) * 0.5

    def diff_y(values):
        return (window(values, 0, 1) - window(values, 0, -1)) * 0.5

    def diff_z(values):
        center = window(values, 0, 0)
        return (shift_z(center, 1, depth) - shift_z(center, -1, depth)) * 0.5

    def middle_sweep_tier(values):
        center = window(values, 0, 0)
        along_x = window(values, 2, 0) - 2.0 * center + window(values, -2, 0)
        along_y = window(values, 0, 2) - 2.0 * center + window(values, 0, -2)
        along_z = shift_z(center, 2, depth) - 2.0 * center + shift_z(center, -2, depth)
        return (along_x + along_y + along_z) * 0.25

    mass = -(diff_x(mom_x) + diff_y(mom_y) + diff_z(mom_z))
    flow_x = -(
        diff_x(mom_x * vel_x + normal_stress_scalar) + diff_y(mom_x * vel_y) + diff_z(mom_x * vel_z)
    ) + DYNAMIC_FRICTION * middle_sweep_tier(vel_x)
    flow_y = -(
        diff_x(mom_y * vel_x) + diff_y(mom_y * vel_y + normal_stress_scalar) + diff_z(mom_y * vel_z)
    ) + DYNAMIC_FRICTION * middle_sweep_tier(vel_y)
    flow_z = -(
        diff_x(mom_z * vel_x) + diff_y(mom_z * vel_y) + diff_z(mom_z * vel_z + normal_stress_scalar)
    ) + DYNAMIC_FRICTION * middle_sweep_tier(vel_z)
    conducted_warmth_current = -(
        diff_x(enthalpy * vel_x) + diff_y(enthalpy * vel_y) + diff_z(enthalpy * vel_z)
    )
    conducted_warmth_current = (
        conducted_warmth_current
        + DYNAMIC_FRICTION * middle_sweep_tier(motion_half_square)
        + CONDUCTIVITY * middle_sweep_tier(gas_warmth_field)
    )
    return jnp.stack([mass, flow_x, flow_y, flow_z, conducted_warmth_current])


def padded_rates(block):
    rows_x = block.shape[1]
    cols_yz = block.shape[2]
    x_padded = with_halo(block.astype(jnp.bfloat16), (("gx", 1),), 2).astype(block.dtype)
    xy_padded = with_halo(x_padded.astype(jnp.bfloat16), (("gy", 2),), 2 * NZ).astype(
        x_padded.dtype
    )

    def window(values, across, along):
        return values[
            2 + across : 2 + across + rows_x, (2 + along) * NZ : (2 + along) * NZ + cols_yz
        ]

    return rates(xy_padded[0], xy_padded[1], xy_padded[2], xy_padded[3], xy_padded[4], window, NZ)


def per_device(fields, stored_rates):
    levels = min(4, lax.axis_size("sec"))
    level_zero = lax.axis_index("sec") % levels == 0
    current = fields[0]
    stored = stored_rates[0]
    for tick_count in range(TICKS):
        arrived = shifted(current.astype(jnp.bfloat16), "sec", 1).astype(current.dtype)
        arrived = jnp.where(level_zero, current, arrived)
        own_rates = padded_rates(current)
        fresh_rates = padded_rates(arrived).astype(jnp.bfloat16)
        quadrature = (
            QUAD_WEIGHTS[0] * stored[0].astype(jnp.float32)
            + QUAD_WEIGHTS[1] * stored[1].astype(jnp.float32)
            + QUAD_WEIGHTS[2] * stored[2].astype(jnp.float32)
            + QUAD_WEIGHTS[3] * fresh_rates.astype(jnp.float32)
        )
        correction = quadrature - stored[2].astype(jnp.float32)
        current = current + TIME_STEP * (
            own_rates + jnp.where(level_zero, jnp.float32(0.0), correction)
        )
        stored = jnp.concatenate([stored[1:], fresh_rates[None]], axis=0)
    return current[None]


def solution(mesh):
    return jax.shard_map(
        per_device,
        mesh=mesh,
        in_specs=(P("sec", None, "gx", "gy"), P("sec", None, None, "gx", "gy")),
        out_specs=P("sec", None, "gx", "gy"),
        check_vma=False,
    )
```

profile of v0, /device:TPU:6, one launch (start us, length us, event | category | flops | bytes accessed | tf_op | source)
XLA Modules:
  0.0 134.4 jit_solution(8496426287091128811)
XLA Ops:
  0.9 4.2 %collective-permute-start.4 = (bf16[5,32,256]{2,1,0:T(8,128)(2,1)S(1)}, bf16[5,32,256]{2,1,0:T(8,128)(2,1)S(1)}, u32[]{:S(2)}, u32[]{:S(2)}) collective-permute-start(bf16[5,32,256]{2,1,0:T(8,128)(2,1)S(1)} %bitcast_convert_fusion), channel_id=1, source_target_pairs={{0,64},{64,128},{128,192},{192,256},{256,320},{320,384},{384,448},... | collective-permute-start | bytes 245768 | tf_op jit(solution)/shard_map/ppermute | solution.py:34
  5.2 2.9 %collective-permute-start.1 = (bf16[5,2,256]{2,1,0:T(2,128)(2,1)S(1)}, bf16[5,2,256]{2,1,0:T(2,128)(2,1)S(1)}, u32[]{:S(2)}, u32[]{:S(2)}) collective-permute-start(bf16[5,2,256]{2,1,0:T(2,128)(2,1)S(1)} %get-tuple-element.208), channel_id=1, source_target_pairs={{4,0},{8,4},{12,8},{16,12},{20,16},{24,20},{28,24},{32,28},{36,32}... | collective-permute-start | bytes 15368 | tf_op jit(solution)/shard_map/ppermute | solution.py:26
  8.1 1.3 collective-permute-done
  9.6 6.1 %collective-permute-start.2 = (bf16[5,36,64]{2,1,0:T(8,128)(2,1)S(1)}, bf16[5,36,64]{2,1,0:T(8,128)(2,1)S(1)}, u32[]{:S(2)}, u32[]{:S(2)}) collective-permute-start(bf16[5,36,64]{2,1,0:T(8,128)(2,1)S(1)} %get-tuple-element.195), channel_id=1, source_target_pairs={{0,1},{1,2},{2,3},{3,0},{4,5},{5,6},{6,7},{7,4},{8,9},{9,10},{10,1... | collective-permute-start | bytes 69128 | tf_op jit(solution)/shard_map/ppermute | solution.py:23
  15.7 5.9 %collective-permute-start.3 = (bf16[5,36,64]{2,1,0:T(8,128)(2,1)S(1)}, bf16[5,36,64]{2,1,0:T(8,128)(2,1)S(1)}, u32[]{:S(2)}, u32[]{:S(2)}) collective-permute-start(bf16[5,36,64]{2,1,0:T(8,128)(2,1)S(1)} %get-tuple-element.196), channel_id=1, source_target_pairs={{1,0},{2,1},{3,2},{0,3},{5,4},{6,5},{7,6},{4,7},{9,8},{10,9},{11,1... | collective-permute-start | bytes 69128 | tf_op jit(solution)/shard_map/ppermute | solution.py:26
  21.6 1.5 %collective-permute-done.2 = bf16[5,36,64]{2,1,0:T(8,128)(2,1)S(1)} collective-permute-done((bf16[5,36,64]{2,1,0:T(8,128)(2,1)S(1)}, bf16[5,36,64]{2,1,0:T(8,128)(2,1)S(1)}, u32[]{:S(2)}, u32[]{:S(2)}) %collective-permute-start.2) | collective-permute-done | bytes 23072 | tf_op jit(solution)/shard_map/ppermute | solution.py:23
  23.1 1.4 %collective-permute-done.3 = bf16[5,36,64]{2,1,0:T(8,128)(2,1)S(1)} collective-permute-done((bf16[5,36,64]{2,1,0:T(8,128)(2,1)S(1)}, bf16[5,36,64]{2,1,0:T(8,128)(2,1)S(1)}, u32[]{:S(2)}, u32[]{:S(2)}) %collective-permute-start.3) | collective-permute-done | bytes 23072 | tf_op jit(solution)/shard_map/ppermute | solution.py:26
  28.8 2.9 %collective-permute-start.6 = (bf16[5,2,256]{2,1,0:T(2,128)(2,1)S(1)}, bf16[5,2,256]{2,1,0:T(2,128)(2,1)S(1)}, u32[]{:S(2)}, u32[]{:S(2)}) collective-permute-start(bf16[5,2,256]{2,1,0:T(2,128)(2,1)S(1)} %get-tuple-element.206), channel_id=1, source_target_pairs={{4,0},{8,4},{12,8},{16,12},{20,16},{24,20},{28,24},{32,28},{36,32}... | collective-permute-start | bytes 15368 | tf_op jit(solution)/shard_map/ppermute | solution.py:26
  33.2 5.7 %collective-permute-start.7 = (bf16[5,36,64]{2,1,0:T(8,128)(2,1)S(1)}, bf16[5,36,64]{2,1,0:T(8,128)(2,1)S(1)}, u32[]{:S(2)}, u32[]{:S(2)}) collective-permute-start(bf16[5,36,64]{2,1,0:T(8,128)(2,1)S(1)} %get-tuple-element.193), channel_id=1, source_target_pairs={{0,1},{1,2},{2,3},{3,0},{4,5},{5,6},{6,7},{7,4},{8,9},{9,10},{10,1... | collective-permute-start | bytes 69128 | tf_op jit(solution)/shard_map/ppermute | solution.py:23
  38.9 2.2 %collective-permute-start.8 = (bf16[5,36,64]{2,1,0:T(8,128)(2,1)S(1)}, bf16[5,36,64]{2,1,0:T(8,128)(2,1)S(1)}, u32[]{:S(2)}, u32[]{:S(2)}) collective-permute-start(bf16[5,36,64]{2,1,0:T(8,128)(2,1)S(1)} %get-tuple-element.194), channel_id=1, source_target_pairs={{1,0},{2,1},{3,2},{0,3},{5,4},{6,5},{7,6},{4,7},{9,8},{10,9},{11,1... | collective-permute-start | bytes 69128 | tf_op jit(solution)/shard_map/ppermute | solution.py:26
  41.7 4.1 %collective-permute-done.8 = bf16[5,36,64]{2,1,0:T(8,128)(2,1)S(1)} collective-permute-done((bf16[5,36,64]{2,1,0:T(8,128)(2,1)S(1)}, bf16[5,36,64]{2,1,0:T(8,128)(2,1)S(1)}, u32[]{:S(2)}, u32[]{:S(2)}) %collective-permute-start.8) | collective-permute-done | bytes 23072 | tf_op jit(solution)/shard_map/ppermute | solution.py:26
  50.5 1.5 %collective-permute-start.10 = (bf16[5,2,256]{2,1,0:T(2,128)(2,1)S(1)}, bf16[5,2,256]{2,1,0:T(2,128)(2,1)S(1)}, u32[]{:S(2)}, u32[]{:S(2)}) collective-permute-start(bf16[5,2,256]{2,1,0:T(2,128)(2,1)S(1)} %get-tuple-element.204), channel_id=1, source_target_pairs={{4,0},{8,4},{12,8},{16,12},{20,16},{24,20},{28,24},{32,28},{36,32}... | collective-permute-start | bytes 15368 | tf_op jit(solution)/shard_map/ppermute | solution.py:26
  52.0 1.3 collective-permute-done.10
  53.4 2.9 %collective-permute-done.9 = bf16[5,2,256]{2,1,0:T(2,128)(2,1)S(1)} collective-permute-done((bf16[5,2,256]{2,1,0:T(2,128)(2,1)S(1)}, bf16[5,2,256]{2,1,0:T(2,128)(2,1)S(1)}, u32[]{:S(2)}, u32[]{:S(2)}) %collective-permute-start.9) | collective-permute-done | bytes 5152 | tf_op jit(solution)/shard_map/ppermute | solution.py:23
  56.4 4.4 %collective-permute-start.11 = (bf16[5,36,64]{2,1,0:T(8,128)(2,1)S(1)}, bf16[5,36,64]{2,1,0:T(8,128)(2,1)S(1)}, u32[]{:S(2)}, u32[]{:S(2)}) collective-permute-start(bf16[5,36,64]{2,1,0:T(8,128)(2,1)S(1)} %get-tuple-element.191), channel_id=1, source_target_pairs={{0,1},{1,2},{2,3},{3,0},{4,5},{5,6},{6,7},{7,4},{8,9},{9,10},{10,1... | collective-permute-start | bytes 69128 | tf_op jit(solution)/shard_map/ppermute | solution.py:23
  60.8 3.5 %collective-permute-start.12 = (bf16[5,36,64]{2,1,0:T(8,128)(2,1)S(1)}, bf16[5,36,64]{2,1,0:T(8,128)(2,1)S(1)}, u32[]{:S(2)}, u32[]{:S(2)}) collective-permute-start(bf16[5,36,64]{2,1,0:T(8,128)(2,1)S(1)} %get-tuple-element.192), channel_id=1, source_target_pairs={{1,0},{2,1},{3,2},{0,3},{5,4},{6,5},{7,6},{4,7},{9,8},{10,9},{11,1... | collective-permute-start | bytes 69128 | tf_op jit(solution)/shard_map/ppermute | solution.py:26
  64.4 5.1 %collective-permute-start.13 = (bf16[5,32,256]{2,1,0:T(8,128)(2,1)S(1)}, bf16[5,32,256]{2,1,0:T(8,128)(2,1)S(1)}, u32[]{:S(2)}, u32[]{:S(2)}) collective-permute-start(bf16[5,32,256]{2,1,0:T(8,128)(2,1)S(1)} %get-tuple-element.59), channel_id=1, source_target_pairs={{0,64},{64,128},{128,192},{192,256},{256,320},{320,384},{384,448},... | collective-permute-start | bytes 245768 | tf_op jit(solution)/shard_map/ppermute | solution.py:34
  74.3 2.9 %collective-permute-start.15 = (bf16[5,2,256]{2,1,0:T(2,128)(2,1)S(1)}, bf16[5,2,256]{2,1,0:T(2,128)(2,1)S(1)}, u32[]{:S(2)}, u32[]{:S(2)}) collective-permute-start(bf16[5,2,256]{2,1,0:T(2,128)(2,1)S(1)} %get-tuple-element.202), channel_id=1, source_target_pairs={{4,0},{8,4},{12,8},{16,12},{20,16},{24,20},{28,24},{32,28},{36,32}... | collective-permute-start | bytes 15368 | tf_op jit(solution)/shard_map/ppermute | solution.py:26
  77.3 1.3 collective-permute-done.14
  78.7 2.2 %collective-permute-start.16 = (bf16[5,36,64]{2,1,0:T(8,128)(2,1)S(1)}, bf16[5,36,64]{2,1,0:T(8,128)(2,1)S(1)}, u32[]{:S(2)}, u32[]{:S(2)}) collective-permute-start(bf16[5,36,64]{2,1,0:T(8,128)(2,1)S(1)} %get-tuple-element.189), channel_id=1, source_target_pairs={{0,1},{1,2},{2,3},{3,0},{4,5},{5,6},{6,7},{7,4},{8,9},{9,10},{10,1... | collective-permute-start | bytes 69128 | tf_op jit(solution)/shard_map/ppermute | solution.py:23
  80.9 5.7 %collective-permute-start.17 = (bf16[5,36,64]{2,1,0:T(8,128)(2,1)S(1)}, bf16[5,36,64]{2,1,0:T(8,128)(2,1)S(1)}, u32[]{:S(2)}, u32[]{:S(2)}) collective-permute-start(bf16[5,36,64]{2,1,0:T(8,128)(2,1)S(1)} %get-tuple-element.190), channel_id=1, source_target_pairs={{1,0},{2,1},{3,2},{0,3},{5,4},{6,5},{7,6},{4,7},{9,8},{10,9},{11,1... | collective-permute-start | bytes 69128 | tf_op jit(solution)/shard_map/ppermute | solution.py:26
  86.8 1.6 %collective-permute-done.17 = bf16[5,36,64]{2,1,0:T(8,128)(2,1)S(1)} collective-permute-done((bf16[5,36,64]{2,1,0:T(8,128)(2,1)S(1)}, bf16[5,36,64]{2,1,0:T(8,128)(2,1)S(1)}, u32[]{:S(2)}, u32[]{:S(2)}) %collective-permute-start.17) | collective-permute-done | bytes 23072 | tf_op jit(solution)/shard_map/ppermute | solution.py:26
  93.3 2.9 %collective-permute-start.19 = (bf16[5,2,256]{2,1,0:T(2,128)(2,1)S(1)}, bf16[5,2,256]{2,1,0:T(2,128)(2,1)S(1)}, u32[]{:S(2)}, u32[]{:S(2)}) collective-permute-start(bf16[5,2,256]{2,1,0:T(2,128)(2,1)S(1)} %get-tuple-element.200), channel_id=1, source_target_pairs={{4,0},{8,4},{12,8},{16,12},{20,16},{24,20},{28,24},{32,28},{36,32}... | collective-permute-start | bytes 15368 | tf_op jit(solution)/shard_map/ppermute | solution.py:26
  96.2 1.3 collective-permute-done.18
  97.7 3.9 %collective-permute-start.20 = (bf16[5,36,64]{2,1,0:T(8,128)(2,1)S(1)}, bf16[5,36,64]{2,1,0:T(8,128)(2,1)S(1)}, u32[]{:S(2)}, u32[]{:S(2)}) collective-permute-start(bf16[5,36,64]{2,1,0:T(8,128)(2,1)S(1)} %get-tuple-element.187), channel_id=1, source_target_pairs={{0,1},{1,2},{2,3},{3,0},{4,5},{5,6},{6,7},{7,4},{8,9},{9,10},{10,1... | collective-permute-start | bytes 69128 | tf_op jit(solution)/shard_map/ppermute | solution.py:23
  101.6 4.4 %collective-permute-start.21 = (bf16[5,36,64]{2,1,0:T(8,128)(2,1)S(1)}, bf16[5,36,64]{2,1,0:T(8,128)(2,1)S(1)}, u32[]{:S(2)}, u32[]{:S(2)}) collective-permute-start(bf16[5,36,64]{2,1,0:T(8,128)(2,1)S(1)} %get-tuple-element.188), channel_id=1, source_target_pairs={{1,0},{2,1},{3,2},{0,3},{5,4},{6,5},{7,6},{4,7},{9,8},{10,9},{11,1... | collective-permute-start | bytes 69128 | tf_op jit(solution)/shard_map/ppermute | solution.py:26
  106.0 3.9 %collective-permute-start.22 = (bf16[5,32,256]{2,1,0:T(8,128)(2,1)S(1)}, bf16[5,32,256]{2,1,0:T(8,128)(2,1)S(1)}, u32[]{:S(2)}, u32[]{:S(2)}) collective-permute-start(bf16[5,32,256]{2,1,0:T(8,128)(2,1)S(1)} %fusion.36), channel_id=1, source_target_pairs={{0,64},{64,128},{128,192},{192,256},{256,320},{320,384},{384,448},... | collective-permute-start | bytes 245768 | tf_op jit(solution)/shard_map/ppermute | solution.py:34
  114.3 2.9 %collective-permute-start.24 = (bf16[5,2,256]{2,1,0:T(2,128)(2,1)S(1)}, bf16[5,2,256]{2,1,0:T(2,128)(2,1)S(1)}, u32[]{:S(2)}, u32[]{:S(2)}) collective-permute-start(bf16[5,2,256]{2,1,0:T(2,128)(2,1)S(1)} %get-tuple-element.198), channel_id=1, source_target_pairs={{4,0},{8,4},{12,8},{16,12},{20,16},{24,20},{28,24},{32,28},{36,32}... | collective-permute-start | bytes 15368 | tf_op jit(solution)/shard_map/ppermute | solution.py:26
  117.3 1.2 collective-permute-done.23
  118.7 2.9 %collective-permute-start.25 = (bf16[5,36,64]{2,1,0:T(8,128)(2,1)S(1)}, bf16[5,36,64]{2,1,0:T(8,128)(2,1)S(1)}, u32[]{:S(2)}, u32[]{:S(2)}) collective-permute-start(bf16[5,36,64]{2,1,0:T(8,128)(2,1)S(1)} %get-tuple-element.185), channel_id=1, source_target_pairs={{0,1},{1,2},{2,3},{3,0},{4,5},{5,6},{6,7},{7,4},{8,9},{9,10},{10,1... | collective-permute-start | bytes 69128 | tf_op jit(solution)/shard_map/ppermute | solution.py:23
  121.6 5.0 %collective-permute-start.26 = (bf16[5,36,64]{2,1,0:T(8,128)(2,1)S(1)}, bf16[5,36,64]{2,1,0:T(8,128)(2,1)S(1)}, u32[]{:S(2)}, u32[]{:S(2)}) collective-permute-start(bf16[5,36,64]{2,1,0:T(8,128)(2,1)S(1)} %get-tuple-element.186), channel_id=1, source_target_pairs={{1,0},{2,1},{3,2},{0,3},{5,4},{6,5},{7,6},{4,7},{9,8},{10,9},{11,1... | collective-permute-start | bytes 69128 | tf_op jit(solution)/shard_map/ppermute | solution.py:26
  127.0 1.9 %collective-permute-done.26 = bf16[5,36,64]{2,1,0:T(8,128)(2,1)S(1)} collective-permute-done((bf16[5,36,64]{2,1,0:T(8,128)(2,1)S(1)}, bf16[5,36,64]{2,1,0:T(8,128)(2,1)S(1)}, u32[]{:S(2)}, u32[]{:S(2)}) %collective-permute-start.26) | collective-permute-done | bytes 23072 | tf_op jit(solution)/shard_map/ppermute | solution.py:26
  (343 shorter events, 31.9 us)
Async XLA Ops:
  0.9 27.2 %collective-permute-start.4 = (bf16[5,32,256]{2,1,0:T(8,128)(2,1)S(1)}, bf16[5,32,256]{2,1,0:T(8,128)(2,1)S(1)}, u32[]{:S(2)}, u32[]{:S(2)}) collective-permute-start(bf16[5,32,256]{2,1,0:T(8,128)(2,1)S(1)} %bitcast_convert_fusion), channel_id=1, source_target_pairs={{0,64},{64,128},{128,192},{192,256},{256,320},{320,384},{384,448},... | collective-permute-start | bytes 245768 | tf_op jit(solution)/shard_map/ppermute | solution.py:34
  5.2 4.3 %collective-permute-start = (bf16[5,2,256]{2,1,0:T(2,128)(2,1)S(1)}, bf16[5,2,256]{2,1,0:T(2,128)(2,1)S(1)}, u32[]{:S(2)}, u32[]{:S(2)}) collective-permute-start(bf16[5,2,256]{2,1,0:T(2,128)(2,1)S(1)} %get-tuple-element.207), channel_id=1, source_target_pairs={{0,4},{4,8},{8,12},{12,16},{16,20},{20,24},{24,28},{28,32},{32,36}... | collective-permute-start | bytes 15368 | tf_op jit(solution)/shard_map/ppermute | solution.py:23
  5.2 4.3 %collective-permute-start.1 = (bf16[5,2,256]{2,1,0:T(2,128)(2,1)S(1)}, bf16[5,2,256]{2,1,0:T(2,128)(2,1)S(1)}, u32[]{:S(2)}, u32[]{:S(2)}) collective-permute-start(bf16[5,2,256]{2,1,0:T(2,128)(2,1)S(1)} %get-tuple-element.208), channel_id=1, source_target_pairs={{4,0},{8,4},{12,8},{16,12},{20,16},{24,20},{28,24},{32,28},{36,32}... | collective-permute-start | bytes 15368 | tf_op jit(solution)/shard_map/ppermute | solution.py:26
  9.6 13.5 %collective-permute-start.2 = (bf16[5,36,64]{2,1,0:T(8,128)(2,1)S(1)}, bf16[5,36,64]{2,1,0:T(8,128)(2,1)S(1)}, u32[]{:S(2)}, u32[]{:S(2)}) collective-permute-start(bf16[5,36,64]{2,1,0:T(8,128)(2,1)S(1)} %get-tuple-element.195), channel_id=1, source_target_pairs={{0,1},{1,2},{2,3},{3,0},{4,5},{5,6},{6,7},{7,4},{8,9},{9,10},{10,1... | collective-permute-start | bytes 69128 | tf_op jit(solution)/shard_map/ppermute | solution.py:23
  15.7 8.8 %collective-permute-start.3 = (bf16[5,36,64]{2,1,0:T(8,128)(2,1)S(1)}, bf16[5,36,64]{2,1,0:T(8,128)(2,1)S(1)}, u32[]{:S(2)}, u32[]{:S(2)}) collective-permute-start(bf16[5,36,64]{2,1,0:T(8,128)(2,1)S(1)} %get-tuple-element.196), channel_id=1, source_target_pairs={{1,0},{2,1},{3,2},{0,3},{5,4},{6,5},{7,6},{4,7},{9,8},{10,9},{11,1... | collective-permute-start | bytes 69128 | tf_op jit(solution)/shard_map/ppermute | solution.py:26
  27.8 0.9 copy-start
  28.8 4.3 %collective-permute-start.5 = (bf16[5,2,256]{2,1,0:T(2,128)(2,1)S(1)}, bf16[5,2,256]{2,1,0:T(2,128)(2,1)S(1)}, u32[]{:S(2)}, u32[]{:S(2)}) collective-permute-start(bf16[5,2,256]{2,1,0:T(2,128)(2,1)S(1)} %get-tuple-element.205), channel_id=1, source_target_pairs={{0,4},{4,8},{8,12},{12,16},{16,20},{20,24},{24,28},{28,32},{32,36}... | collective-permute-start | bytes 15368 | tf_op jit(solution)/shard_map/ppermute | solution.py:23
  28.8 4.3 %collective-permute-start.6 = (bf16[5,2,256]{2,1,0:T(2,128)(2,1)S(1)}, bf16[5,2,256]{2,1,0:T(2,128)(2,1)S(1)}, u32[]{:S(2)}, u32[]{:S(2)}) collective-permute-start(bf16[5,2,256]{2,1,0:T(2,128)(2,1)S(1)} %get-tuple-element.206), channel_id=1, source_target_pairs={{4,0},{8,4},{12,8},{16,12},{20,16},{24,20},{28,24},{32,28},{36,32}... | collective-permute-start | bytes 15368 | tf_op jit(solution)/shard_map/ppermute | solution.py:26
  33.2 8.5 %collective-permute-start.7 = (bf16[5,36,64]{2,1,0:T(8,128)(2,1)S(1)}, bf16[5,36,64]{2,1,0:T(8,128)(2,1)S(1)}, u32[]{:S(2)}, u32[]{:S(2)}) collective-permute-start(bf16[5,36,64]{2,1,0:T(8,128)(2,1)S(1)} %get-tuple-element.193), channel_id=1, source_target_pairs={{0,1},{1,2},{2,3},{3,0},{4,5},{5,6},{6,7},{7,4},{8,9},{9,10},{10,1... | collective-permute-start | bytes 69128 | tf_op jit(solution)/shard_map/ppermute | solution.py:23
  38.9 6.9 %collective-permute-start.8 = (bf16[5,36,64]{2,1,0:T(8,128)(2,1)S(1)}, bf16[5,36,64]{2,1,0:T(8,128)(2,1)S(1)}, u32[]{:S(2)}, u32[]{:S(2)}) collective-permute-start(bf16[5,36,64]{2,1,0:T(8,128)(2,1)S(1)} %get-tuple-element.194), channel_id=1, source_target_pairs={{1,0},{2,1},{3,2},{0,3},{5,4},{6,5},{7,6},{4,7},{9,8},{10,9},{11,1... | collective-permute-start | bytes 69128 | tf_op jit(solution)/shard_map/ppermute | solution.py:26
  49.4 0.9 copy-start.1
  50.5 2.9 %collective-permute-start.10 = (bf16[5,2,256]{2,1,0:T(2,128)(2,1)S(1)}, bf16[5,2,256]{2,1,0:T(2,128)(2,1)S(1)}, u32[]{:S(2)}, u32[]{:S(2)}) collective-permute-start(bf16[5,2,256]{2,1,0:T(2,128)(2,1)S(1)} %get-tuple-element.204), channel_id=1, source_target_pairs={{4,0},{8,4},{12,8},{16,12},{20,16},{24,20},{28,24},{32,28},{36,32}... | collective-permute-start | bytes 15368 | tf_op jit(solution)/shard_map/ppermute | solution.py:26
  52.0 4.3 %collective-permute-start.9 = (bf16[5,2,256]{2,1,0:T(2,128)(2,1)S(1)}, bf16[5,2,256]{2,1,0:T(2,128)(2,1)S(1)}, u32[]{:S(2)}, u32[]{:S(2)}) collective-permute-start(bf16[5,2,256]{2,1,0:T(2,128)(2,1)S(1)} %get-tuple-element.203), channel_id=1, source_target_pairs={{0,4},{4,8},{8,12},{12,16},{16,20},{20,24},{24,28},{28,32},{32,36}... | collective-permute-start | bytes 15368 | tf_op jit(solution)/shard_map/ppermute | solution.py:23
  56.4 13.1 %collective-permute-start.11 = (bf16[5,36,64]{2,1,0:T(8,128)(2,1)S(1)}, bf16[5,36,64]{2,1,0:T(8,128)(2,1)S(1)}, u32[]{:S(2)}, u32[]{:S(2)}) collective-permute-start(bf16[5,36,64]{2,1,0:T(8,128)(2,1)S(1)} %get-tuple-element.191), channel_id=1, source_target_pairs={{0,1},{1,2},{2,3},{3,0},{4,5},{5,6},{6,7},{7,4},{8,9},{9,10},{10,1... | collective-permute-start | bytes 69128 | tf_op jit(solution)/shard_map/ppermute | solution.py:23
  60.8 8.7 %collective-permute-start.12 = (bf16[5,36,64]{2,1,0:T(8,128)(2,1)S(1)}, bf16[5,36,64]{2,1,0:T(8,128)(2,1)S(1)}, u32[]{:S(2)}, u32[]{:S(2)}) collective-permute-start(bf16[5,36,64]{2,1,0:T(8,128)(2,1)S(1)} %get-tuple-element.192), channel_id=1, source_target_pairs={{1,0},{2,1},{3,2},{0,3},{5,4},{6,5},{7,6},{4,7},{9,8},{10,9},{11,1... | collective-permute-start | bytes 69128 | tf_op jit(solution)/shard_map/ppermute | solution.py:26
  64.4 9.8 %collective-permute-start.13 = (bf16[5,32,256]{2,1,0:T(8,128)(2,1)S(1)}, bf16[5,32,256]{2,1,0:T(8,128)(2,1)S(1)}, u32[]{:S(2)}, u32[]{:S(2)}) collective-permute-start(bf16[5,32,256]{2,1,0:T(8,128)(2,1)S(1)} %get-tuple-element.59), channel_id=1, source_target_pairs={{0,64},{64,128},{128,192},{192,256},{256,320},{320,384},{384,448},... | collective-permute-start | bytes 245768 | tf_op jit(solution)/shard_map/ppermute | solution.py:34
  74.3 4.3 %collective-permute-start.14 = (bf16[5,2,256]{2,1,0:T(2,128)(2,1)S(1)}, bf16[5,2,256]{2,1,0:T(2,128)(2,1)S(1)}, u32[]{:S(2)}, u32[]{:S(2)}) collective-permute-start(bf16[5,2,256]{2,1,0:T(2,128)(2,1)S(1)} %get-tuple-element.201), channel_id=1, source_target_pairs={{0,4},{4,8},{8,12},{12,16},{16,20},{20,24},{24,28},{28,32},{32,36}... | collective-permute-start | bytes 15368 | tf_op jit(solution)/shard_map/ppermute | solution.py:23
  74.3 4.3 %collective-permute-start.15 = (bf16[5,2,256]{2,1,0:T(2,128)(2,1)S(1)}, bf16[5,2,256]{2,1,0:T(2,128)(2,1)S(1)}, u32[]{:S(2)}, u32[]{:S(2)}) collective-permute-start(bf16[5,2,256]{2,1,0:T(2,128)(2,1)S(1)} %get-tuple-element.202), channel_id=1, source_target_pairs={{4,0},{8,4},{12,8},{16,12},{20,16},{24,20},{28,24},{32,28},{36,32}... | collective-permute-start | bytes 15368 | tf_op jit(solution)/shard_map/ppermute | solution.py:26
  78.7 8.1 %collective-permute-start.16 = (bf16[5,36,64]{2,1,0:T(8,128)(2,1)S(1)}, bf16[5,36,64]{2,1,0:T(8,128)(2,1)S(1)}, u32[]{:S(2)}, u32[]{:S(2)}) collective-permute-start(bf16[5,36,64]{2,1,0:T(8,128)(2,1)S(1)} %get-tuple-element.189), channel_id=1, source_target_pairs={{0,1},{1,2},{2,3},{3,0},{4,5},{5,6},{6,7},{7,4},{8,9},{9,10},{10,1... | collective-permute-start | bytes 69128 | tf_op jit(solution)/shard_map/ppermute | solution.py:23
  80.9 7.5 %collective-permute-start.17 = (bf16[5,36,64]{2,1,0:T(8,128)(2,1)S(1)}, bf16[5,36,64]{2,1,0:T(8,128)(2,1)S(1)}, u32[]{:S(2)}, u32[]{:S(2)}) collective-permute-start(bf16[5,36,64]{2,1,0:T(8,128)(2,1)S(1)} %get-tuple-element.190), channel_id=1, source_target_pairs={{1,0},{2,1},{3,2},{0,3},{5,4},{6,5},{7,6},{4,7},{9,8},{10,9},{11,1... | collective-permute-start | bytes 69128 | tf_op jit(solution)/shard_map/ppermute | solution.py:26
  93.3 4.3 %collective-permute-start.18 = (bf16[5,2,256]{2,1,0:T(2,128)(2,1)S(1)}, bf16[5,2,256]{2,1,0:T(2,128)(2,1)S(1)}, u32[]{:S(2)}, u32[]{:S(2)}) collective-permute-start(bf16[5,2,256]{2,1,0:T(2,128)(2,1)S(1)} %get-tuple-element.199), channel_id=1, source_target_pairs={{0,4},{4,8},{8,12},{12,16},{16,20},{20,24},{24,28},{28,32},{32,36}... | collective-permute-start | bytes 15368 | tf_op jit(solution)/shard_map/ppermute | solution.py:23
  93.3 4.3 %collective-permute-start.19 = (bf16[5,2,256]{2,1,0:T(2,128)(2,1)S(1)}, bf16[5,2,256]{2,1,0:T(2,128)(2,1)S(1)}, u32[]{:S(2)}, u32[]{:S(2)}) collective-permute-start(bf16[5,2,256]{2,1,0:T(2,128)(2,1)S(1)} %get-tuple-element.200), channel_id=1, source_target_pairs={{4,0},{8,4},{12,8},{16,12},{20,16},{24,20},{28,24},{32,28},{36,32}... | collective-permute-start | bytes 15368 | tf_op jit(solution)/shard_map/ppermute | solution.py:26
  97.7 12.2 %collective-permute-start.20 = (bf16[5,36,64]{2,1,0:T(8,128)(2,1)S(1)}, bf16[5,36,64]{2,1,0:T(8,128)(2,1)S(1)}, u32[]{:S(2)}, u32[]{:S(2)}) collective-permute-start(bf16[5,36,64]{2,1,0:T(8,128)(2,1)S(1)} %get-tuple-element.187), channel_id=1, source_target_pairs={{0,1},{1,2},{2,3},{3,0},{4,5},{5,6},{6,7},{7,4},{8,9},{9,10},{10,1... | collective-permute-start | bytes 69128 | tf_op jit(solution)/shard_map/ppermute | solution.py:23
  101.6 8.3 %collective-permute-start.21 = (bf16[5,36,64]{2,1,0:T(8,128)(2,1)S(1)}, bf16[5,36,64]{2,1,0:T(8,128)(2,1)S(1)}, u32[]{:S(2)}, u32[]{:S(2)}) collective-permute-start(bf16[5,36,64]{2,1,0:T(8,128)(2,1)S(1)} %get-tuple-element.188), channel_id=1, source_target_pairs={{1,0},{2,1},{3,2},{0,3},{5,4},{6,5},{7,6},{4,7},{9,8},{10,9},{11,1... | collective-permute-start | bytes 69128 | tf_op jit(solution)/shard_map/ppermute | solution.py:26
  106.0 8.2 %collective-permute-start.22 = (bf16[5,32,256]{2,1,0:T(8,128)(2,1)S(1)}, bf16[5,32,256]{2,1,0:T(8,128)(2,1)S(1)}, u32[]{:S(2)}, u32[]{:S(2)}) collective-permute-start(bf16[5,32,256]{2,1,0:T(8,128)(2,1)S(1)} %fusion.36), channel_id=1, source_target_pairs={{0,64},{64,128},{128,192},{192,256},{256,320},{320,384},{384,448},... | collective-permute-start | bytes 245768 | tf_op jit(solution)/shard_map/ppermute | solution.py:34
  114.3 4.3 %collective-permute-start.23 = (bf16[5,2,256]{2,1,0:T(2,128)(2,1)S(1)}, bf16[5,2,256]{2,1,0:T(2,128)(2,1)S(1)}, u32[]{:S(2)}, u32[]{:S(2)}) collective-permute-start(bf16[5,2,256]{2,1,0:T(2,128)(2,1)S(1)} %get-tuple-element.197), channel_id=1, source_target_pairs={{0,4},{4,8},{8,12},{12,16},{16,20},{20,24},{24,28},{28,32},{32,36}... | collective-permute-start | bytes 15368 | tf_op jit(solution)/shard_map/ppermute | solution.py:23
  114.3 4.3 %collective-permute-start.24 = (bf16[5,2,256]{2,1,0:T(2,128)(2,1)S(1)}, bf16[5,2,256]{2,1,0:T(2,128)(2,1)S(1)}, u32[]{:S(2)}, u32[]{:S(2)}) collective-permute-start(bf16[5,2,256]{2,1,0:T(2,128)(2,1)S(1)} %get-tuple-element.198), channel_id=1, source_target_pairs={{4,0},{8,4},{12,8},{16,12},{20,16},{24,20},{28,24},{32,28},{36,32}... | collective-permute-start | bytes 15368 | tf_op jit(solution)/shard_map/ppermute | solution.py:26
  118.7 8.3 %collective-permute-start.25 = (bf16[5,36,64]{2,1,0:T(8,128)(2,1)S(1)}, bf16[5,36,64]{2,1,0:T(8,128)(2,1)S(1)}, u32[]{:S(2)}, u32[]{:S(2)}) collective-permute-start(bf16[5,36,64]{2,1,0:T(8,128)(2,1)S(1)} %get-tuple-element.185), channel_id=1, source_target_pairs={{0,1},{1,2},{2,3},{3,0},{4,5},{5,6},{6,7},{7,4},{8,9},{9,10},{10,1... | collective-permute-start | bytes 69128 | tf_op jit(solution)/shard_map/ppermute | solution.py:23
  121.6 7.2 %collective-permute-start.26 = (bf16[5,36,64]{2,1,0:T(8,128)(2,1)S(1)}, bf16[5,36,64]{2,1,0:T(8,128)(2,1)S(1)}, u32[]{:S(2)}, u32[]{:S(2)}) collective-permute-start(bf16[5,36,64]{2,1,0:T(8,128)(2,1)S(1)} %get-tuple-element.186), channel_id=1, source_target_pairs={{1,0},{2,1},{3,2},{0,3},{5,4},{6,5},{7,6},{4,7},{9,8},{10,9},{11,1... | collective-permute-start | bytes 69128 | tf_op jit(solution)/shard_map/ppermute | solution.py:26
where the time goes:
time: 137 us; the launch traced here: 134 us
  starting transfers between devices  81.6 us (60%)
  waiting for transfers between devices  21.9 us (16%)
  local copies, waits for them, and re-layouts  20 us (15%)
  other arithmetic  9.86 us (7%)
    ppermute x12, starting transfers between devices, with_halo(): lax.ppermute(lax.slice_in_dim(block, 0, width, axis=dim), axis, backward)  43 us
    ppermute x12, starting transfers between devices, with_halo(): lax.ppermute(lax.slice_in_dim(block, block.shape[dim] - width, None, axis...  25.4 us
    ppermute x3, starting transfers between devices, shifted(): return lax.ppermute(block, axis, route)  13.2 us
    ppermute x12, waiting for transfers between devices, with_halo(): lax.ppermute(lax.slice_in_dim(block, block.shape[dim] - width, None, axis...  11.3 us
    ppermute x12, waiting for transfers between devices, with_halo(): lax.ppermute(lax.slice_in_dim(block, 0, width, axis=dim), axis, backward)  10.6 us
    slice x108, local copies, waits for them, and re-layouts, shift_z(): unwrapped = jnp.roll(values, -step, axis=-1)  8.98 us
    slice x88, local copies, waits for them, and re-layouts, shift_z(): wrapped = jnp.roll(values, depth - step, axis=-1)  7.33 us
    unnamed x24, other arithmetic  4.3 us
  transfers between devices with their start and end apart: 27, of which 14 were waited for; matrix products, arithmetic and copies ran while one was open for 10% of the time, Pallas kernels for 0%

commit v1 on v0

v1 whole, which is shorter than its diff:
```python
import jax
import jax.numpy as jnp
from jax import lax
from jax.experimental import pallas as pl
from jax.experimental.pallas import tpu as pltpu
from jax.sharding import PartitionSpec as P

NZ = 32
TICKS = 3
LEVELS = 4
TIME_STEP = 0.04
DYNAMIC_FRICTION = 0.4
CONDUCTIVITY = 0.5
GAMMA_LESS = 0.4
W0, W1, W2, W3 = 1.0 / 24.0, -5.0 / 24.0, 19.0 / 24.0 - 1.0, 9.0 / 24.0
MESH = pl.DeviceIdType.MESH


def primitives(density, mom_x, mom_y, mom_z, energy):
    inverse = 1.0 / density
    vel = (mom_x * inverse, mom_y * inverse, mom_z * inverse)
    kinetic = 0.5 * (vel[0] * vel[0] + vel[1] * vel[1] + vel[2] * vel[2])
    pressure = GAMMA_LESS * (energy - density * kinetic)
    heat = DYNAMIC_FRICTION * kinetic + CONDUCTIVITY * (pressure * inverse)
    return (mom_x, mom_y, mom_z), vel, pressure, energy + pressure, heat


def flux_difference(axis, prims, difference):
    mom, vel, pressure, enthalpy, heat = prims
    terms = [difference(mom[axis]) * -0.5]
    for c in range(3):
        flux = mom[c] * vel[axis]
        if c == axis:
            flux = flux + pressure
        spread = difference(vel[c]) * (0.5 * DYNAMIC_FRICTION)
        terms.append(difference(spread - flux) * 0.5)
    spread = difference(heat) * 0.5
    terms.append(difference(spread - enthalpy * vel[axis]) * 0.5)
    return terms


def ring_difference(axis, step):
    def difference(values):
        size = values.shape[axis]
        return pltpu.roll(values, size - step, axis) - pltpu.roll(values, step, axis)

    return difference


def z_difference(values):
    lane = lax.broadcasted_iota(jnp.int32, values.shape, 1) % NZ
    up = jnp.where(
        lane < NZ - 1, pltpu.roll(values, 127, 1), pltpu.roll(values, NZ - 1, 1)
    )
    down = jnp.where(lane > 0, pltpu.roll(values, 1, 1), pltpu.roll(values, 129 - NZ, 1))
    return up - down


def tree_concat(first, second, axis):
    return jax.tree.map(lambda a, b: jnp.concatenate([a, b], axis=axis), first, second)


def kernel(
    counts, fields, stored, out, u, st, rate, x_lo, x_hi, y_send, y_lo, y_hi,
    f_send, f_recv, load_sem, x_ss, x_rs, y_ss, y_rs, f_ss, f_rs,
):
    n_sec, n_gx, n_gy = counts
    sec, gx, gy = lax.axis_index("sec"), lax.axis_index("gx"), lax.axis_index("gy")
    level = lax.rem(sec, LEVELS)
    gx_up, gx_down = lax.rem(gx + 1, n_gx), lax.rem(gx + n_gx - 1, n_gx)
    gy_up, gy_down = lax.rem(gy + 1, n_gy), lax.rem(gy + n_gy - 1, n_gy)
    sec_up, sec_down = lax.rem(sec + 1, n_sec), lax.rem(sec + n_sec - 1, n_sec)
    has_up, has_down = level < LEVELS - 1, level > 0

    load_u = pltpu.make_async_copy(fields.at[0], u.at[0], load_sem.at[0])
    load_st = pltpu.make_async_copy(stored.at[0], st, load_sem.at[1])
    load_u.start()
    load_st.start()

    barrier = pltpu.get_barrier_semaphore()
    for target in ({"gx": gx_up}, {"gx": gx_down}, {"gy": gy_up}, {"gy": gy_down}):
        pl.semaphore_signal(barrier, inc=1, device_id=target, device_id_type=MESH)

    @pl.when(has_up)
    def _():
        pl.semaphore_signal(barrier, inc=1, device_id={"sec": sec_up}, device_id_type=MESH)

    @pl.when(has_down)
    def _():
        pl.semaphore_signal(barrier, inc=1, device_id={"sec": sec_down}, device_id_type=MESH)

    load_u.wait()

    def remote(src, dst, send, recv, target):
        return pltpu.make_async_remote_copy(
            src_ref=src, dst_ref=dst, send_sem=send, recv_sem=recv,
            device_id=target, device_id_type=MESH,
        )

    lane = lax.broadcasted_iota(jnp.int32, (16, 128), 1)
    row = lax.broadcasted_iota(jnp.int32, (8, 256), 0)
    copies = []
    for tick in range(TICKS):
        now = u.at[tick]
        for f in range(5):
            first, last = now[f, :, 0:128], now[f, :, 128:256]
            y_send[tick, 0, f] = jnp.where(
                lane < 64, first[0:16], pltpu.roll(first[16:32], 64, 1)
            ).astype(jnp.bfloat16)
            y_send[tick, 1, f] = jnp.where(
                lane < 64, pltpu.roll(last[16:32], 64, 1), last[0:16]
            ).astype(jnp.bfloat16)
        if tick == 0:
            pl.semaphore_wait(
                barrier, 4 + has_up.astype(jnp.int32) + has_down.astype(jnp.int32)
            )
        to_y = (
            remote(y_send.at[tick, 0], y_hi.at[tick], y_ss.at[tick, 0], y_rs.at[tick, 0], {"gy": gy_down}),
            remote(y_send.at[tick, 1], y_lo.at[tick], y_ss.at[tick, 1], y_rs.at[tick, 1], {"gy": gy_up}),
        )
        to_x = (
            remote(now.at[:, 0:8], x_hi.at[tick], x_ss.at[tick, 0], x_rs.at[tick, 0], {"gx": gx_down}),
            remote(now.at[:, 24:32], x_lo.at[tick], x_ss.at[tick, 1], x_rs.at[tick, 1], {"gx": gx_up}),
        )
        for copy in to_y + to_x:
            copy.start()
        copies += to_y + to_x

        for half in range(2):
            cols = slice(128 * half, 128 * half + 128)
            prims = primitives(*(now[f, :, cols] for f in range(5)))
            for f, term in enumerate(flux_difference(2, prims, z_difference)):
                rate[f, :, cols] = term

        main = primitives(*(now[f] for f in range(5)))
        for copy in to_x:
            copy.wait_recv()
        halo = primitives(
            *(jnp.where(row < 4, x_hi[tick, f], x_lo[tick, f]) for f in range(5))
        )
        ring = tree_concat(main, halo, 0)
        for f, term in enumerate(flux_difference(0, ring, ring_difference(0, 1))):
            rate[f] += term[0:32]

        for copy in to_y:
            copy.wait_recv()
        sides = []
        for f in range(5):
            high = y_hi[tick, f].astype(jnp.float32)
            low = y_lo[tick, f].astype(jnp.float32)
            top = jnp.where(lane < 64, high, low)
            bottom = pltpu.roll(jnp.where(lane < 64, low, high), 64, 1)
            sides.append(jnp.concatenate([top, bottom], axis=0))
        ring = tree_concat(main, primitives(*sides), 1)
        terms = flux_difference(1, ring, ring_difference(1, NZ))
        for f, term in enumerate(terms):
            own = rate[f] + term[:, 0:256]
            rate[f] = own
            f_send[tick, f] = own.astype(jnp.bfloat16)

        to_next = remote(
            f_send.at[tick], f_recv.at[tick], f_ss.at[tick], f_rs.at[tick], {"sec": sec_up}
        )

        @pl.when(has_up)
        def _():
            to_next.start()

        if tick == 0:
            load_st.wait()
        target = out.at[0] if tick == TICKS - 1 else u.at[tick + 1]

        @pl.when(level == 0)
        def _():
            for f in range(5):
                target[f] = now[f] + TIME_STEP * rate[f]

        @pl.when(has_down)
        def _():
            history = [st.at[h] for h in range(3)] + [f_recv.at[h] for h in range(tick)]
            a, b, c = history[tick : tick + 3]
            for f in range(5):
                known = (
                    W0 * a[f].astype(jnp.float32)
                    + W1 * b[f].astype(jnp.float32)
                    + W2 * c[f].astype(jnp.float32)
                )
                rate[f] = now[f] + TIME_STEP * (rate[f] + known)
            to_next.wait_recv()
            for f in range(5):
                target[f] = rate[f] + (TIME_STEP * W3) * f_recv[tick, f].astype(jnp.float32)

        @pl.when(has_up)
        def _():
            to_next.wait_send()

    for copy in copies:
        copy.wait_send()


def solution(mesh):
    counts = tuple(mesh.shape[name] for name in ("sec", "gx", "gy"))

    def per_device(fields, stored_rates):
        _, _, rows, cols = fields.shape
        halo_x = pltpu.VMEM((TICKS, 5, 8, cols), jnp.float32)
        halo_y = pltpu.VMEM((TICKS, 5, rows // 2, 128), jnp.bfloat16)
        block = (5, rows, cols)
        return pl.pallas_call(
            lambda *refs: kernel(counts, *refs),
            name="correct",
            out_shape=jax.ShapeDtypeStruct(fields.shape, fields.dtype),
            in_specs=[pl.BlockSpec(memory_space=pl.ANY)] * 2,
            out_specs=pl.BlockSpec(memory_space=pltpu.VMEM),
            scratch_shapes=[
                pltpu.VMEM((TICKS,) + block, jnp.float32),
                pltpu.VMEM((3,) + block, jnp.bfloat16),
                pltpu.VMEM(block, jnp.float32),
                halo_x,
                halo_x,
                pltpu.VMEM((TICKS, 2, 5, rows // 2, 128), jnp.bfloat16),
                halo_y,
                halo_y,
                pltpu.VMEM((TICKS,) + block, jnp.bfloat16),
                pltpu.VMEM((TICKS,) + block, jnp.bfloat16),
                pltpu.SemaphoreType.DMA((2,)),
                pltpu.SemaphoreType.DMA((TICKS, 2)),
                pltpu.SemaphoreType.DMA((TICKS, 2)),
                pltpu.SemaphoreType.DMA((TICKS, 2)),
                pltpu.SemaphoreType.DMA((TICKS, 2)),
                pltpu.SemaphoreType.DMA((TICKS,)),
                pltpu.SemaphoreType.DMA((TICKS,)),
            ],
            compiler_params=pltpu.CompilerParams(collective_id=0, has_side_effects=True),
        )(fields, stored_rates)

    return jax.shard_map(
        per_device,
        mesh=mesh,
        in_specs=(P("sec", None, "gx", "gy"), P("sec", None, None, "gx", "gy")),
        out_specs=P("sec", None, "gx", "gy"),
        check_vma=False,
    )
```

time: 137 us -> 35.8 us (0.26); the launches traced: 134 us -> 35.5 us
  starting transfers between devices: 81.6 us -> 0 us
  Pallas kernels: 0 us -> 33.9 us
  waiting for transfers between devices: 21.9 us -> 0 us
  local copies, waits for them, and re-layouts: 20 us -> 1.59 us
  other arithmetic: 9.86 us -> 0 us
    ppermute x27 -> x0, starting transfers between devices: 81.6 us -> none  [the longest x12 43 us: with_halo(): lax.ppermute(lax.slice_in_dim(block, 0, width, axis=dim), axis, backward)]
    pallas_call x0 -> x1, Pallas kernels: none -> 33.9 us  [per_device(): pl.pallas_call(lambda *refs: kernel(counts, *refs), name='correct', out_s...]
    ppermute x27 -> x0, waiting for transfers between devices: 21.9 us -> none  [the longest x12 11.3 us: with_halo(): lax.ppermute(lax.slice_in_dim(block, block.shape[dim] - width, None, axis...]
    slice x228 -> x0, local copies, waits for them, and re-layouts: 18.5 us -> none  [the longest x108 8.98 us: shift_z(): unwrapped = jnp.roll(values, -step, axis=-1)]
    unnamed x24 -> x0, other arithmetic: 4.3 us -> none
    convert_element_type x11 -> x0, other arithmetic: 1.97 us -> none  [the longest x5 1.08 us: padded_rates(): block.astype(jnp.bfloat16)]
    another operation x6 -> x0, other arithmetic: 1.66 us -> none  [rates(): return jnp.stack([mass, flow_x, flow_y, flow_z, conducted_warmth_current])]
  transfers between devices with their start and end apart: 27 -> 0, of which waited for: 14 -> 0; matrix products, arithmetic and copies ran while one was open for 10% -> 0% of each run, Pallas kernels for 0% -> 0%
where the time goes in v1:
time: 35.8 us; the launch traced here: 35.5 us
  Pallas kernels  33.9 us (95%)
  local copies, waits for them, and re-layouts  1.59 us (4%)
    pallas_call x1, Pallas kernels, per_device(): pl.pallas_call(lambda *refs: kernel(counts, *refs), name='correct', out_s...  33.9 us
    unnamed x1, local copies, waits for them, and re-layouts  1.59 us

profile of v1, /device:TPU:6, one launch (start us, length us, event | category | flops | bytes accessed | tf_op | source)
XLA Modules:
  0.0 35.5 jit_solution(10960409402127899153)
XLA Ops:
  0.0 33.9 %correct.1 = f32[1,5,32,256]{3,2,1,0:T(8,128)} custom-call(f32[1,5,32,256]{3,2,1,0:T(8,128)} %refs_0_.1, bf16[1,3,5,32,256]{4,3,2,1,0:T(8,128)(2,1)} %refs_1_.1), custom_call_target="tpu_custom_call" | custom-call | tf_op jit(solution)/shard_map/correct/pallas_call | solution.py:209
  33.9 1.6 %copy.4 = f32[1,5,32,256]{3,2,1,0:T(8,128)} copy(f32[1,5,32,256]{3,2,1,0:T(8,128)} %correct.1) | data formatting | bytes 327680

commit v2 on v1

--- a/solution.py
+++ b/solution.py
@@ -61,7 +61,7 @@
 
 
 def kernel(
-    counts, fields, stored, out, u, st, rate, x_lo, x_hi, y_send, y_lo, y_hi,
+    counts, fields, stored, out, u, st, rate, inside, x_lo, x_hi, y_send, y_lo, y_hi,
     f_send, f_recv, load_sem, x_ss, x_rs, y_ss, y_rs, f_ss, f_rs,
 ):
     n_sec, n_gx, n_gy = counts
@@ -99,6 +99,11 @@
 
     lane = lax.broadcasted_iota(jnp.int32, (16, 128), 1)
     row = lax.broadcasted_iota(jnp.int32, (8, 256), 0)
+
+    def fresh(tick, f):
+        halves = [f_recv[tick, h, f].astype(jnp.float32) for h in range(2)]
+        return pltpu.roll(jnp.concatenate(halves, axis=1), 64, 1)
+
     copies = []
     for tick in range(TICKS):
         now = u.at[tick]
@@ -133,6 +138,9 @@
                 rate[f, :, cols] = term
 
         main = primitives(*(now[f] for f in range(5)))
+        inner = flux_difference(1, main, ring_difference(1, NZ))
+        for f in range(5):
+            inside[f] = pltpu.roll(inner[f], 192, 1)[:, 0:128]
         for copy in to_x:
             copy.wait_recv()
         halo = primitives(
@@ -140,7 +148,23 @@
         )
         ring = tree_concat(main, halo, 0)
         for f, term in enumerate(flux_difference(0, ring, ring_difference(0, 1))):
-            rate[f] += term[0:32]
+            part = rate[f] + term[0:32]
+            rate[f] = part
+            whole = pltpu.roll(part, 192, 1)[:, 0:128] + inside[f]
+            inside[f] = whole
+            f_send[tick, 0, f] = whole.astype(jnp.bfloat16)
+
+        to_next = [
+            remote(
+                f_send.at[tick, h], f_recv.at[tick, h], f_ss.at[tick, h], f_rs.at[tick, h],
+                {"sec": sec_up},
+            )
+            for h in range(2)
+        ]
+
+        @pl.when(has_up)
+        def _():
+            to_next[0].start()
 
         for copy in to_y:
             copy.wait_recv()
@@ -156,15 +180,11 @@
         for f, term in enumerate(terms):
             own = rate[f] + term[:, 0:256]
             rate[f] = own
-            f_send[tick, f] = own.astype(jnp.bfloat16)
-
-        to_next = remote(
-            f_send.at[tick], f_recv.at[tick], f_ss.at[tick], f_rs.at[tick], {"sec": sec_up}
-        )
+            f_send[tick, 1, f] = pltpu.roll(own, 64, 1)[:, 0:128].astype(jnp.bfloat16)
 
         @pl.when(has_up)
         def _():
-            to_next.start()
+            to_next[1].start()
 
         if tick == 0:
             load_st.wait()
@@ -177,22 +197,21 @@
 
         @pl.when(has_down)
         def _():
-            history = [st.at[h] for h in range(3)] + [f_recv.at[h] for h in range(tick)]
-            a, b, c = history[tick : tick + 3]
+            def past(h, f):
+                return st[h, f].astype(jnp.float32) if h < 3 else fresh(h - 3, f)
+
             for f in range(5):
-                known = (
-                    W0 * a[f].astype(jnp.float32)
-                    + W1 * b[f].astype(jnp.float32)
-                    + W2 * c[f].astype(jnp.float32)
-                )
+                known = W0 * past(tick, f) + W1 * past(tick + 1, f) + W2 * past(tick + 2, f)
                 rate[f] = now[f] + TIME_STEP * (rate[f] + known)
-            to_next.wait_recv()
+            for copy in to_next:
+                copy.wait_recv()
             for f in range(5):
-                target[f] = rate[f] + (TIME_STEP * W3) * f_recv[tick, f].astype(jnp.float32)
+                target[f] = rate[f] + (TIME_STEP * W3) * fresh(tick, f)
 
         @pl.when(has_up)
         def _():
-            to_next.wait_send()
+            for copy in to_next:
+                copy.wait_send()
 
     for copy in copies:
         copy.wait_send()
@@ -206,6 +225,7 @@
         halo_x = pltpu.VMEM((TICKS, 5, 8, cols), jnp.float32)
         halo_y = pltpu.VMEM((TICKS, 5, rows // 2, 128), jnp.bfloat16)
         block = (5, rows, cols)
+        level_half = pltpu.VMEM((TICKS, 2, 5, rows, 128), jnp.bfloat16)
         return pl.pallas_call(
             lambda *refs: kernel(counts, *refs),
             name="correct",
@@ -216,20 +236,21 @@
                 pltpu.VMEM((TICKS,) + block, jnp.float32),
                 pltpu.VMEM((3,) + block, jnp.bfloat16),
                 pltpu.VMEM(block, jnp.float32),
+                pltpu.VMEM((5, rows, 128), jnp.float32),
                 halo_x,
                 halo_x,
                 pltpu.VMEM((TICKS, 2, 5, rows // 2, 128), jnp.bfloat16),
                 halo_y,
                 halo_y,
-                pltpu.VMEM((TICKS,) + block, jnp.bfloat16),
-                pltpu.VMEM((TICKS,) + block, jnp.bfloat16),
+                level_half,
+                level_half,
                 pltpu.SemaphoreType.DMA((2,)),
                 pltpu.SemaphoreType.DMA((TICKS, 2)),
                 pltpu.SemaphoreType.DMA((TICKS, 2)),
                 pltpu.SemaphoreType.DMA((TICKS, 2)),
                 pltpu.SemaphoreType.DMA((TICKS, 2)),
-                pltpu.SemaphoreType.DMA((TICKS,)),
-                pltpu.SemaphoreType.DMA((TICKS,)),
+                pltpu.SemaphoreType.DMA((TICKS, 2)),
+                pltpu.SemaphoreType.DMA((TICKS, 2)),
             ],
             compiler_params=pltpu.CompilerParams(collective_id=0, has_side_effects=True),
         )(fields, stored_rates)

time: 35.8 us -> 34.3 us (0.958)
  Pallas kernels: 33.9 us -> 32.6 us
    pallas_call x1, Pallas kernels: 33.9 us -> 32.6 us  [per_device(): pl.pallas_call(lambda *refs: kernel(counts, *refs), name='correct', out_s...]
where the time goes in v2:
time: 34.3 us; the launch traced here: 34.2 us
  Pallas kernels  32.6 us (95%)
  local copies, waits for them, and re-layouts  1.59 us (5%)
    pallas_call x1, Pallas kernels, per_device(): pl.pallas_call(lambda *refs: kernel(counts, *refs), name='correct', out_s...  32.6 us
    unnamed x1, local copies, waits for them, and re-layouts  1.59 us

profile of v2, /device:TPU:6, one launch (start us, length us, event | category | flops | bytes accessed | tf_op | source)
XLA Modules:
  0.0 34.2 jit_solution(219747637897708047)
XLA Ops:
  0.0 32.6 %correct.1 = f32[1,5,32,256]{3,2,1,0:T(8,128)} custom-call(f32[1,5,32,256]{3,2,1,0:T(8,128)} %refs_0_.1, bf16[1,3,5,32,256]{4,3,2,1,0:T(8,128)(2,1)} %refs_1_.1), custom_call_target="tpu_custom_call" | custom-call | tf_op jit(solution)/shard_map/correct/pallas_call | solution.py:229
  32.6 1.6 %copy.4 = f32[1,5,32,256]{3,2,1,0:T(8,128)} copy(f32[1,5,32,256]{3,2,1,0:T(8,128)} %correct.1) | data formatting | bytes 327680

commit v3 on v2

--- a/solution.py
+++ b/solution.py
@@ -56,12 +56,27 @@
     return up - down
 
 
-def tree_concat(first, second, axis):
-    return jax.tree.map(lambda a, b: jnp.concatenate([a, b], axis=axis), first, second)
+def halo_terms(axis, prims, cell, array_axis, step):
+    mom, vel, pressure, enthalpy, heat = prims
+    size = cell.shape[array_axis]
+
+    def outer(flux):
+        after = pltpu.roll(flux, step, array_axis)
+        before = pltpu.roll(flux, size - step, array_axis)
+        return jnp.where(cell == 1, -0.5 * after, jnp.where(cell == 6, 0.5 * before, 0.0))
+
+    terms = [outer(mom[axis])]
+    for c in range(3):
+        flux = mom[c] * vel[axis]
+        if c == axis:
+            flux = flux + pressure
+        terms.append(outer(flux) + (0.25 * DYNAMIC_FRICTION) * vel[c])
+    terms.append(outer(enthalpy * vel[axis]) + 0.25 * heat)
+    return terms
 
 
 def kernel(
-    counts, fields, stored, out, u, st, rate, inside, x_lo, x_hi, y_send, y_lo, y_hi,
+    counts, fields, stored, out, u, st, rate, x_lo, x_hi, y_send, y_lo, y_hi,
     f_send, f_recv, load_sem, x_ss, x_rs, y_ss, y_rs, f_ss, f_rs,
 ):
     n_sec, n_gx, n_gy = counts
@@ -99,6 +114,9 @@
 
     lane = lax.broadcasted_iota(jnp.int32, (16, 128), 1)
     row = lax.broadcasted_iota(jnp.int32, (8, 256), 0)
+    lane_all = lax.broadcasted_iota(jnp.int32, (32, 128), 1)
+    side = lane_all // NZ
+    side = jnp.where(side < 2, side, side + 4)
 
     def fresh(tick, f):
         halves = [f_recv[tick, h, f].astype(jnp.float32) for h in range(2)]
@@ -136,23 +154,26 @@
             prims = primitives(*(now[f, :, cols] for f in range(5)))
             for f, term in enumerate(flux_difference(2, prims, z_difference)):
                 rate[f, :, cols] = term
-
         main = primitives(*(now[f] for f in range(5)))
-        inner = flux_difference(1, main, ring_difference(1, NZ))
-        for f in range(5):
-            inside[f] = pltpu.roll(inner[f], 192, 1)[:, 0:128]
+        for axis, array_axis, step in ((0, 0, 1), (1, 1, NZ)):
+            zeros = jnp.zeros((8, 256) if axis == 0 else (32, 128), jnp.float32)
+            ring = jax.tree.map(
+                lambda v: jnp.concatenate([v, zeros], axis=array_axis), main
+            )
+            terms = flux_difference(axis, ring, ring_difference(array_axis, step))
+            for f in range(5):
+                rate[f] += terms[f][0:32, 0:256]
+
         for copy in to_x:
             copy.wait_recv()
-        halo = primitives(
+        prims = primitives(
             *(jnp.where(row < 4, x_hi[tick, f], x_lo[tick, f]) for f in range(5))
         )
-        ring = tree_concat(main, halo, 0)
-        for f, term in enumerate(flux_difference(0, ring, ring_difference(0, 1))):
-            part = rate[f] + term[0:32]
-            rate[f] = part
-            whole = pltpu.roll(part, 192, 1)[:, 0:128] + inside[f]
-            inside[f] = whole
-            f_send[tick, 0, f] = whole.astype(jnp.bfloat16)
+        for f, term in enumerate(halo_terms(0, prims, row, 0, 1)):
+            rate[f, 0:8] += jnp.where(row < 2, pltpu.roll(term, 2, 0), 0.0)
+            rate[f, 24:32] += jnp.where(row >= 6, pltpu.roll(term, 6, 0), 0.0)
+        for f in range(5):
+            f_send[tick, 0, f] = pltpu.roll(rate[f], 192, 1)[:, 0:128].astype(jnp.bfloat16)
 
         to_next = [
             remote(
@@ -175,16 +196,19 @@
             top = jnp.where(lane < 64, high, low)
             bottom = pltpu.roll(jnp.where(lane < 64, low, high), 64, 1)
             sides.append(jnp.concatenate([top, bottom], axis=0))
-        ring = tree_concat(main, primitives(*sides), 1)
-        terms = flux_difference(1, ring, ring_difference(1, NZ))
-        for f, term in enumerate(terms):
-            own = rate[f] + term[:, 0:256]
-            rate[f] = own
-            f_send[tick, 1, f] = pltpu.roll(own, 64, 1)[:, 0:128].astype(jnp.bfloat16)
+        edges = halo_terms(1, primitives(*sides), side, 1, NZ)
+        for f in range(5):
+            own = pltpu.roll(rate[f], 64, 1)[:, 0:128] + edges[f]
+            f_send[tick, 1, f] = own.astype(jnp.bfloat16)
 
         @pl.when(has_up)
         def _():
             to_next[1].start()
+
+        for f in range(5):
+            edge = pltpu.roll(edges[f], 64, 1)
+            rate[f, :, 0:128] += jnp.where(lane_all < 64, edge, 0.0)
+            rate[f, :, 128:256] += jnp.where(lane_all >= 64, edge, 0.0)
 
         if tick == 0:
             load_st.wait()
@@ -229,14 +253,13 @@
         return pl.pallas_call(
             lambda *refs: kernel(counts, *refs),
             name="correct",
-            out_shape=jax.ShapeDtypeStruct(fields.shape, fields.dtype),
+            out_shape=pltpu.VMEM(fields.shape, fields.dtype),
             in_specs=[pl.BlockSpec(memory_space=pl.ANY)] * 2,
             out_specs=pl.BlockSpec(memory_space=pltpu.VMEM),
             scratch_shapes=[
                 pltpu.VMEM((TICKS,) + block, jnp.float32),
                 pltpu.VMEM((3,) + block, jnp.bfloat16),
                 pltpu.VMEM(block, jnp.float32),
-                pltpu.VMEM((5, rows, 128), jnp.float32),
                 halo_x,
                 halo_x,
                 pltpu.VMEM((TICKS, 2, 5, rows // 2, 128), jnp.bfloat16),

time: 34.3 us -> 32.1 us (0.936)
  Pallas kernels: 32.6 us -> 31.3 us
  local copies, waits for them, and re-layouts: 1.59 us -> 0.67 us
    pallas_call x1, Pallas kernels: 32.6 us -> 31.3 us  [per_device(): pl.pallas_call(lambda *refs: kernel(counts, *refs), name='correct', out_s...]
    unnamed x1, local copies, waits for them, and re-layouts: 1.59 us -> 0.67 us
where the time goes in v3:
time: 32.1 us; the launch traced here: 32 us
  Pallas kernels  31.3 us (98%)
  local copies, waits for them, and re-layouts  0.67 us (2%)
    pallas_call x1, Pallas kernels, per_device(): pl.pallas_call(lambda *refs: kernel(counts, *refs), name='correct', out_s...  31.3 us
    unnamed x1, local copies, waits for them, and re-layouts  0.67 us

profile of v3, /device:TPU:6, one launch (start us, length us, event | category | flops | bytes accessed | tf_op | source)
XLA Modules:
  0.0 32.0 jit_solution(5916629674307542123)
XLA Ops:
  0.0 31.3 %correct.1 = f32[1,5,32,256]{3,2,1,0:T(8,128)S(1)} custom-call(f32[1,5,32,256]{3,2,1,0:T(8,128)} %refs_0_.1, bf16[1,3,5,32,256]{4,3,2,1,0:T(8,128)(2,1)} %refs_1_.1), custom_call_target="tpu_custom_call" | custom-call | tf_op jit(solution)/shard_map/correct/pallas_call | solution.py:253
  31.3 0.7 %copy.4 = f32[1,5,32,256]{3,2,1,0:T(8,128)} copy(f32[1,5,32,256]{3,2,1,0:T(8,128)S(1)} %correct.1) | data formatting | bytes 327680

commit v4 on v3

--- a/solution.py
+++ b/solution.py
@@ -77,7 +77,8 @@
 
 def kernel(
     counts, fields, stored, out, u, st, rate, x_lo, x_hi, y_send, y_lo, y_hi,
-    f_send, f_recv, load_sem, x_ss, x_rs, y_ss, y_rs, f_ss, f_rs,
+    f_send, f_recv, c_send, c_recv, d_lo, d_hi, past_fresh,
+    load_sem, x_ss, x_rs, y_ss, y_rs, f_ss, f_rs, c_ss, c_rs, d_ss, d_rs,
 ):
     n_sec, n_gx, n_gy = counts
     sec, gx, gy = lax.axis_index("sec"), lax.axis_index("gx"), lax.axis_index("gy")
@@ -98,11 +99,13 @@
 
     @pl.when(has_up)
     def _():
-        pl.semaphore_signal(barrier, inc=1, device_id={"sec": sec_up}, device_id_type=MESH)
+        for target in ({"sec": sec_up}, {"sec": sec_up, "gy": gy_up}, {"sec": sec_up, "gy": gy_down}):
+            pl.semaphore_signal(barrier, inc=1, device_id=target, device_id_type=MESH)
 
     @pl.when(has_down)
     def _():
-        pl.semaphore_signal(barrier, inc=1, device_id={"sec": sec_down}, device_id_type=MESH)
+        for target in ({"sec": sec_down}, {"sec": sec_down, "gy": gy_up}, {"sec": sec_down, "gy": gy_down}):
+            pl.semaphore_signal(barrier, inc=1, device_id=target, device_id_type=MESH)
 
     load_u.wait()
 
@@ -118,11 +121,26 @@
     side = lane_all // NZ
     side = jnp.where(side < 2, side, side + 4)
 
-    def fresh(tick, f):
-        halves = [f_recv[tick, h, f].astype(jnp.float32) for h in range(2)]
-        return pltpu.roll(jnp.concatenate(halves, axis=1), 64, 1)
-
-    copies = []
+    def y_edges(low, high):
+        sides = []
+        for f in range(5):
+            above, below = high[f].astype(jnp.float32), low[f].astype(jnp.float32)
+            top = jnp.where(lane < 64, above, below)
+            bottom = pltpu.roll(jnp.where(lane < 64, below, above), 64, 1)
+            sides.append(jnp.concatenate([top, bottom], axis=0))
+        return halo_terms(1, primitives(*sides), side, 1, NZ)
+
+    def add_y(to, edges):
+        for f in range(5):
+            edge = pltpu.roll(edges[f], 64, 1)
+            to[f, :, 0:128] += jnp.where(lane_all < 64, edge, 0.0)
+            to[f, :, 128:256] += jnp.where(lane_all >= 64, edge, 0.0)
+
+    def add_x(to, f, term):
+        to[f, 0:8] += jnp.where(row < 2, pltpu.roll(term, 2, 0), 0.0)
+        to[f, 24:32] += jnp.where(row >= 6, pltpu.roll(term, 6, 0), 0.0)
+
+    copies, up_copies = [], ()
     for tick in range(TICKS):
         now = u.at[tick]
         for f in range(5):
@@ -135,7 +153,7 @@
             ).astype(jnp.bfloat16)
         if tick == 0:
             pl.semaphore_wait(
-                barrier, 4 + has_up.astype(jnp.int32) + has_down.astype(jnp.int32)
+                barrier, 4 + 3 * has_up.astype(jnp.int32) + 3 * has_down.astype(jnp.int32)
             )
         to_y = (
             remote(y_send.at[tick, 0], y_hi.at[tick], y_ss.at[tick, 0], y_rs.at[tick, 0], {"gy": gy_down}),
@@ -145,9 +163,26 @@
             remote(now.at[:, 0:8], x_hi.at[tick], x_ss.at[tick, 0], x_rs.at[tick, 0], {"gx": gx_down}),
             remote(now.at[:, 24:32], x_lo.at[tick], x_ss.at[tick, 1], x_rs.at[tick, 1], {"gx": gx_up}),
         )
+        diagonal = (
+            remote(y_send.at[tick, 0], d_hi.at[tick], d_ss.at[tick, 0], d_rs.at[tick, 0], {"sec": sec_up, "gy": gy_down}),
+            remote(y_send.at[tick, 1], d_lo.at[tick], d_ss.at[tick, 1], d_rs.at[tick, 1], {"sec": sec_up, "gy": gy_up}),
+        )
+        to_next = remote(
+            f_send.at[tick], f_recv.at[tick], f_ss.at[tick], f_rs.at[tick], {"sec": sec_up}
+        )
+        x_next = remote(
+            c_send.at[tick], c_recv.at[tick], c_ss.at[tick], c_rs.at[tick], {"sec": sec_up}
+        )
         for copy in to_y + to_x:
             copy.start()
+
+        @pl.when(has_up)
+        def _():
+            for copy in diagonal:
+                copy.start()
+
         copies += to_y + to_x
+        up_copies += (to_next, x_next) + diagonal
 
         for half in range(2):
             cols = slice(128 * half, 128 * half + 128)
@@ -162,7 +197,14 @@
             )
             terms = flux_difference(axis, ring, ring_difference(array_axis, step))
             for f in range(5):
-                rate[f] += terms[f][0:32, 0:256]
+                total = rate[f] + terms[f][0:32, 0:256]
+                rate[f] = total
+                if axis == 1:
+                    f_send[tick, f] = total.astype(jnp.bfloat16)
+
+        @pl.when(has_up)
+        def _():
+            to_next.start()
 
         for copy in to_x:
             copy.wait_recv()
@@ -170,45 +212,16 @@
             *(jnp.where(row < 4, x_hi[tick, f], x_lo[tick, f]) for f in range(5))
         )
         for f, term in enumerate(halo_terms(0, prims, row, 0, 1)):
-            rate[f, 0:8] += jnp.where(row < 2, pltpu.roll(term, 2, 0), 0.0)
-            rate[f, 24:32] += jnp.where(row >= 6, pltpu.roll(term, 6, 0), 0.0)
-        for f in range(5):
-            f_send[tick, 0, f] = pltpu.roll(rate[f], 192, 1)[:, 0:128].astype(jnp.bfloat16)
-
-        to_next = [
-            remote(
-                f_send.at[tick, h], f_recv.at[tick, h], f_ss.at[tick, h], f_rs.at[tick, h],
-                {"sec": sec_up},
-            )
-            for h in range(2)
-        ]
+            c_send[tick, f] = term.astype(jnp.bfloat16)
+            add_x(rate, f, term)
 
         @pl.when(has_up)
         def _():
-            to_next[0].start()
+            x_next.start()
 
         for copy in to_y:
             copy.wait_recv()
-        sides = []
-        for f in range(5):
-            high = y_hi[tick, f].astype(jnp.float32)
-            low = y_lo[tick, f].astype(jnp.float32)
-            top = jnp.where(lane < 64, high, low)
-            bottom = pltpu.roll(jnp.where(lane < 64, low, high), 64, 1)
-            sides.append(jnp.concatenate([top, bottom], axis=0))
-        edges = halo_terms(1, primitives(*sides), side, 1, NZ)
-        for f in range(5):
-            own = pltpu.roll(rate[f], 64, 1)[:, 0:128] + edges[f]
-            f_send[tick, 1, f] = own.astype(jnp.bfloat16)
-
-        @pl.when(has_up)
-        def _():
-            to_next[1].start()
-
-        for f in range(5):
-            edge = pltpu.roll(edges[f], 64, 1)
-            rate[f, :, 0:128] += jnp.where(lane_all < 64, edge, 0.0)
-            rate[f, :, 128:256] += jnp.where(lane_all >= 64, edge, 0.0)
+        add_y(rate, y_edges(y_lo[tick], y_hi[tick]))
 
         if tick == 0:
             load_st.wait()
@@ -222,20 +235,28 @@
         @pl.when(has_down)
         def _():
             def past(h, f):
-                return st[h, f].astype(jnp.float32) if h < 3 else fresh(h - 3, f)
+                return st[h, f].astype(jnp.float32) if h < 3 else past_fresh[h - 3, f]
 
             for f in range(5):
                 known = W0 * past(tick, f) + W1 * past(tick + 1, f) + W2 * past(tick + 2, f)
                 rate[f] = now[f] + TIME_STEP * (rate[f] + known)
-            for copy in to_next:
+            new = past_fresh.at[tick]
+            to_next.wait_recv()
+            for f in range(5):
+                new[f] = f_recv[tick, f].astype(jnp.float32)
+            x_next.wait_recv()
+            for f in range(5):
+                add_x(new, f, c_recv[tick, f].astype(jnp.float32))
+            for copy in diagonal:
                 copy.wait_recv()
-            for f in range(5):
-                target[f] = rate[f] + (TIME_STEP * W3) * fresh(tick, f)
-
-        @pl.when(has_up)
-        def _():
-            for copy in to_next:
-                copy.wait_send()
+            add_y(new, y_edges(d_lo[tick], d_hi[tick]))
+            for f in range(5):
+                target[f] = rate[f] + (TIME_STEP * W3) * new[f]
+
+    @pl.when(has_up)
+    def _():
+        for copy in up_copies:
+            copy.wait_send()
 
     for copy in copies:
         copy.wait_send()
@@ -249,7 +270,8 @@
         halo_x = pltpu.VMEM((TICKS, 5, 8, cols), jnp.float32)
         halo_y = pltpu.VMEM((TICKS, 5, rows // 2, 128), jnp.bfloat16)
         block = (5, rows, cols)
-        level_half = pltpu.VMEM((TICKS, 2, 5, rows, 128), jnp.bfloat16)
+        level_block = pltpu.VMEM((TICKS,) + block, jnp.bfloat16)
+        x_terms = pltpu.VMEM((TICKS, 5, 8, cols), jnp.bfloat16)
         return pl.pallas_call(
             lambda *refs: kernel(counts, *refs),
             name="correct",
@@ -265,13 +287,22 @@
                 pltpu.VMEM((TICKS, 2, 5, rows // 2, 128), jnp.bfloat16),
                 halo_y,
                 halo_y,
-                level_half,
-                level_half,
+                level_block,
+                level_block,
+                x_terms,
+                x_terms,
+                halo_y,
+                halo_y,
+                pltpu.VMEM((TICKS,) + block, jnp.float32),
                 pltpu.SemaphoreType.DMA((2,)),
                 pltpu.SemaphoreType.DMA((TICKS, 2)),
                 pltpu.SemaphoreType.DMA((TICKS, 2)),
                 pltpu.SemaphoreType.DMA((TICKS, 2)),
                 pltpu.SemaphoreType.DMA((TICKS, 2)),
+                pltpu.SemaphoreType.DMA((TICKS,)),
+                pltpu.SemaphoreType.DMA((TICKS,)),
+                pltpu.SemaphoreType.DMA((TICKS,)),
+                pltpu.SemaphoreType.DMA((TICKS,)),
                 pltpu.SemaphoreType.DMA((TICKS, 2)),
                 pltpu.SemaphoreType.DMA((TICKS, 2)),
             ],

time: 32.1 us -> 30.5 us (0.950)
  Pallas kernels: 31.3 us -> 29.7 us
    pallas_call x1, Pallas kernels: 31.3 us -> 29.7 us  [per_device(): pl.pallas_call(lambda *refs: kernel(counts, *refs), name='correct', out_s...]
where the time goes in v4:
time: 30.5 us; the launch traced here: 30.3 us
  Pallas kernels  29.7 us (97%)
  local copies, waits for them, and re-layouts  0.67 us (2%)
    pallas_call x1, Pallas kernels, per_device(): pl.pallas_call(lambda *refs: kernel(counts, *refs), name='correct', out_s...  29.7 us
    unnamed x1, local copies, waits for them, and re-layouts  0.67 us

profile of v4, /device:TPU:6, one launch (start us, length us, event | category | flops | bytes accessed | tf_op | source)
XLA Modules:
  0.0 30.3 jit_solution(13271777966182848107)
XLA Ops:
  0.0 29.7 %correct.1 = f32[1,5,32,256]{3,2,1,0:T(8,128)S(1)} custom-call(f32[1,5,32,256]{3,2,1,0:T(8,128)} %refs_0_.1, bf16[1,3,5,32,256]{4,3,2,1,0:T(8,128)(2,1)} %refs_1_.1), custom_call_target="tpu_custom_call" | custom-call | tf_op jit(solution)/shard_map/correct/pallas_call | solution.py:275
  29.7 0.7 %copy.4 = f32[1,5,32,256]{3,2,1,0:T(8,128)} copy(f32[1,5,32,256]{3,2,1,0:T(8,128)S(1)} %correct.1) | data formatting | bytes 327680

commit v5 on v4

--- a/solution.py
+++ b/solution.py
@@ -211,14 +211,20 @@
         prims = primitives(
             *(jnp.where(row < 4, x_hi[tick, f], x_lo[tick, f]) for f in range(5))
         )
-        for f, term in enumerate(halo_terms(0, prims, row, 0, 1)):
-            c_send[tick, f] = term.astype(jnp.bfloat16)
-            add_x(rate, f, term)
+        ends = halo_terms(0, prims, row, 0, 1)
+        for pair in range(3):
+            tile = ends[2 * pair]
+            if pair < 2:
+                inner = jnp.logical_and(row >= 2, row < 6)
+                tile = jnp.where(inner, pltpu.roll(ends[2 * pair + 1], 4, 0), tile)
+            c_send[tick, pair] = tile.astype(jnp.bfloat16)
 
         @pl.when(has_up)
         def _():
             x_next.start()
 
+        for f in range(5):
+            add_x(rate, f, ends[f])
         for copy in to_y:
             copy.wait_recv()
         add_y(rate, y_edges(y_lo[tick], y_hi[tick]))
@@ -241,17 +247,25 @@
                 known = W0 * past(tick, f) + W1 * past(tick + 1, f) + W2 * past(tick + 2, f)
                 rate[f] = now[f] + TIME_STEP * (rate[f] + known)
             new = past_fresh.at[tick]
-            to_next.wait_recv()
-            for f in range(5):
-                new[f] = f_recv[tick, f].astype(jnp.float32)
-            x_next.wait_recv()
-            for f in range(5):
-                add_x(new, f, c_recv[tick, f].astype(jnp.float32))
             for copy in diagonal:
                 copy.wait_recv()
-            add_y(new, y_edges(d_lo[tick], d_hi[tick]))
-            for f in range(5):
-                target[f] = rate[f] + (TIME_STEP * W3) * new[f]
+            edges = y_edges(d_lo[tick], d_hi[tick])
+            for f in range(5):
+                edge = pltpu.roll(edges[f], 64, 1)
+                new[f, :, 0:128] = jnp.where(lane_all < 64, edge, 0.0)
+                new[f, :, 128:256] = jnp.where(lane_all >= 64, edge, 0.0)
+            to_next.wait_recv()
+            for f in range(5):
+                whole = new[f] + f_recv[tick, f].astype(jnp.float32)
+                new[f] = whole
+                target[f] = rate[f] + (TIME_STEP * W3) * whole
+            x_next.wait_recv()
+            for f in range(5):
+                term = c_recv[tick, f // 2].astype(jnp.float32)
+                if f % 2:
+                    term = pltpu.roll(term, 4, 0)
+                add_x(target, f, (TIME_STEP * W3) * term)
+                add_x(new, f, term)
 
     @pl.when(has_up)
     def _():
@@ -271,7 +285,7 @@
         halo_y = pltpu.VMEM((TICKS, 5, rows // 2, 128), jnp.bfloat16)
         block = (5, rows, cols)
         level_block = pltpu.VMEM((TICKS,) + block, jnp.bfloat16)
-        x_terms = pltpu.VMEM((TICKS, 5, 8, cols), jnp.bfloat16)
+        x_terms = pltpu.VMEM((TICKS, 3, 8, cols), jnp.bfloat16)
         return pl.pallas_call(
             lambda *refs: kernel(counts, *refs),
             name="correct",

time: 30.5 us -> 29.4 us (0.964)
  Pallas kernels: 29.7 us -> 28.6 us
    pallas_call x1, Pallas kernels: 29.7 us -> 28.6 us  [per_device(): pl.pallas_call(lambda *refs: kernel(counts, *refs), name='correct', out_s...]
where the time goes in v5:
time: 29.4 us; the launch traced here: 29.3 us
  Pallas kernels  28.6 us (97%)
  local copies, waits for them, and re-layouts  0.67 us (2%)
    pallas_call x1, Pallas kernels, per_device(): pl.pallas_call(lambda *refs: kernel(counts, *refs), name='correct', out_s...  28.6 us
    unnamed x1, local copies, waits for them, and re-layouts  0.67 us

profile of v5, /device:TPU:6, one launch (start us, length us, event | category | flops | bytes accessed | tf_op | source)
XLA Modules:
  0.0 29.3 jit_solution(1648190053112299521)
XLA Ops:
  0.0 28.6 %correct.1 = f32[1,5,32,256]{3,2,1,0:T(8,128)S(1)} custom-call(f32[1,5,32,256]{3,2,1,0:T(8,128)} %refs_0_.1, bf16[1,3,5,32,256]{4,3,2,1,0:T(8,128)(2,1)} %refs_1_.1), custom_call_target="tpu_custom_call" | custom-call | tf_op jit(solution)/shard_map/correct/pallas_call | solution.py:289
  28.6 0.7 %copy.4 = f32[1,5,32,256]{3,2,1,0:T(8,128)} copy(f32[1,5,32,256]{3,2,1,0:T(8,128)S(1)} %correct.1) | data formatting | bytes 327680

commit v6 on v5

--- a/solution.py
+++ b/solution.py
@@ -27,16 +27,15 @@
 
 def flux_difference(axis, prims, difference):
     mom, vel, pressure, enthalpy, heat = prims
-    terms = [difference(mom[axis]) * -0.5]
+    yield difference(mom[axis]) * -0.5
     for c in range(3):
         flux = mom[c] * vel[axis]
         if c == axis:
             flux = flux + pressure
         spread = difference(vel[c]) * (0.5 * DYNAMIC_FRICTION)
-        terms.append(difference(spread - flux) * 0.5)
+        yield difference(spread - flux) * 0.5
     spread = difference(heat) * 0.5
-    terms.append(difference(spread - enthalpy * vel[axis]) * 0.5)
-    return terms
+    yield difference(spread - enthalpy * vel[axis]) * 0.5
 
 
 def ring_difference(axis, step):
@@ -94,9 +93,6 @@
     load_st.start()
 
     barrier = pltpu.get_barrier_semaphore()
-    for target in ({"gx": gx_up}, {"gx": gx_down}, {"gy": gy_up}, {"gy": gy_down}):
-        pl.semaphore_signal(barrier, inc=1, device_id=target, device_id_type=MESH)
-
     @pl.when(has_up)
     def _():
         for target in ({"sec": sec_up}, {"sec": sec_up, "gy": gy_up}, {"sec": sec_up, "gy": gy_down}):
@@ -106,6 +102,9 @@
     def _():
         for target in ({"sec": sec_down}, {"sec": sec_down, "gy": gy_up}, {"sec": sec_down, "gy": gy_down}):
             pl.semaphore_signal(barrier, inc=1, device_id=target, device_id_type=MESH)
+
+    for target in ({"gx": gx_up}, {"gx": gx_down}, {"gy": gy_up}, {"gy": gy_down}):
+        pl.semaphore_signal(barrier, inc=1, device_id=target, device_id_type=MESH)
 
     load_u.wait()
 
@@ -167,22 +166,26 @@
             remote(y_send.at[tick, 0], d_hi.at[tick], d_ss.at[tick, 0], d_rs.at[tick, 0], {"sec": sec_up, "gy": gy_down}),
             remote(y_send.at[tick, 1], d_lo.at[tick], d_ss.at[tick, 1], d_rs.at[tick, 1], {"sec": sec_up, "gy": gy_up}),
         )
-        to_next = remote(
-            f_send.at[tick], f_recv.at[tick], f_ss.at[tick], f_rs.at[tick], {"sec": sec_up}
+        to_next = tuple(
+            remote(
+                f_send.at[tick, f], f_recv.at[tick, f], f_ss.at[tick, f], f_rs.at[tick, f],
+                {"sec": sec_up},
+            )
+            for f in range(5)
         )
         x_next = remote(
             c_send.at[tick], c_recv.at[tick], c_ss.at[tick], c_rs.at[tick], {"sec": sec_up}
         )
-        for copy in to_y + to_x:
-            copy.start()
-
         @pl.when(has_up)
         def _():
             for copy in diagonal:
                 copy.start()
 
+        for copy in to_y + to_x:
+            copy.start()
+
         copies += to_y + to_x
-        up_copies += (to_next, x_next) + diagonal
+        up_copies += to_next + (x_next,) + diagonal
 
         for half in range(2):
             cols = slice(128 * half, 128 * half + 128)
@@ -196,15 +199,12 @@
                 lambda v: jnp.concatenate([v, zeros], axis=array_axis), main
             )
             terms = flux_difference(axis, ring, ring_difference(array_axis, step))
-            for f in range(5):
-                total = rate[f] + terms[f][0:32, 0:256]
+            for f, term in enumerate(terms):
+                total = rate[f] + term[0:32, 0:256]
                 rate[f] = total
                 if axis == 1:
                     f_send[tick, f] = total.astype(jnp.bfloat16)
-
-        @pl.when(has_up)
-        def _():
-            to_next.start()
+                    pl.when(has_up)(to_next[f].start)
 
         for copy in to_x:
             copy.wait_recv()
@@ -254,8 +254,8 @@
                 edge = pltpu.roll(edges[f], 64, 1)
                 new[f, :, 0:128] = jnp.where(lane_all < 64, edge, 0.0)
                 new[f, :, 128:256] = jnp.where(lane_all >= 64, edge, 0.0)
-            to_next.wait_recv()
-            for f in range(5):
+            for f in range(5):
+                to_next[f].wait_recv()
                 whole = new[f] + f_recv[tick, f].astype(jnp.float32)
                 new[f] = whole
                 target[f] = rate[f] + (TIME_STEP * W3) * whole
@@ -313,8 +313,8 @@
                 pltpu.SemaphoreType.DMA((TICKS, 2)),
                 pltpu.SemaphoreType.DMA((TICKS, 2)),
                 pltpu.SemaphoreType.DMA((TICKS, 2)),
-                pltpu.SemaphoreType.DMA((TICKS,)),
-                pltpu.SemaphoreType.DMA((TICKS,)),
+                pltpu.SemaphoreType.DMA((TICKS, 5)),
+                pltpu.SemaphoreType.DMA((TICKS, 5)),
                 pltpu.SemaphoreType.DMA((TICKS,)),
                 pltpu.SemaphoreType.DMA((TICKS,)),
                 pltpu.SemaphoreType.DMA((TICKS, 2)),

time: 29.4 us -> 29.5 us (level)
  no operation moved by 1% of the time
where the time goes in v6:
time: 29.5 us; the launch traced here: 29.4 us
  Pallas kernels  28.7 us (97%)
  local copies, waits for them, and re-layouts  0.67 us (2%)
    pallas_call x1, Pallas kernels, per_device(): pl.pallas_call(lambda *refs: kernel(counts, *refs), name='correct', out_s...  28.7 us
    unnamed x1, local copies, waits for them, and re-layouts  0.67 us

profile of v6, /device:TPU:6, one launch (start us, length us, event | category | flops | bytes accessed | tf_op | source)
XLA Modules:
  0.0 29.4 jit_solution(7134250484597275468)
XLA Ops:
  0.0 28.7 %correct.1 = f32[1,5,32,256]{3,2,1,0:T(8,128)S(1)} custom-call(f32[1,5,32,256]{3,2,1,0:T(8,128)} %refs_0_.1, bf16[1,3,5,32,256]{4,3,2,1,0:T(8,128)(2,1)} %refs_1_.1), custom_call_target="tpu_custom_call" | custom-call | tf_op jit(solution)/shard_map/correct/pallas_call | solution.py:289
  28.8 0.7 %copy.4 = f32[1,5,32,256]{3,2,1,0:T(8,128)} copy(f32[1,5,32,256]{3,2,1,0:T(8,128)S(1)} %correct.1) | data formatting | bytes 327680

commit v7 on v6

--- a/solution.py
+++ b/solution.py
@@ -247,16 +247,9 @@
                 known = W0 * past(tick, f) + W1 * past(tick + 1, f) + W2 * past(tick + 2, f)
                 rate[f] = now[f] + TIME_STEP * (rate[f] + known)
             new = past_fresh.at[tick]
-            for copy in diagonal:
-                copy.wait_recv()
-            edges = y_edges(d_lo[tick], d_hi[tick])
-            for f in range(5):
-                edge = pltpu.roll(edges[f], 64, 1)
-                new[f, :, 0:128] = jnp.where(lane_all < 64, edge, 0.0)
-                new[f, :, 128:256] = jnp.where(lane_all >= 64, edge, 0.0)
             for f in range(5):
                 to_next[f].wait_recv()
-                whole = new[f] + f_recv[tick, f].astype(jnp.float32)
+                whole = f_recv[tick, f].astype(jnp.float32)
                 new[f] = whole
                 target[f] = rate[f] + (TIME_STEP * W3) * whole
             x_next.wait_recv()
@@ -266,6 +259,12 @@
                     term = pltpu.roll(term, 4, 0)
                 add_x(target, f, (TIME_STEP * W3) * term)
                 add_x(new, f, term)
+            for copy in diagonal:
+                copy.wait_recv()
+            edges = y_edges(d_lo[tick], d_hi[tick])
+            add_y(target, [(TIME_STEP * W3) * edge for edge in edges])
+            if tick < TICKS - 1:
+                add_y(new, edges)
 
     @pl.when(has_up)
     def _():

time: 29.5 us -> 30.4 us (1.031)
  Pallas kernels: 28.7 us -> 29.6 us
    pallas_call x1, Pallas kernels: 28.7 us -> 29.6 us  [per_device(): pl.pallas_call(lambda *refs: kernel(counts, *refs), name='correct', out_s...]
where the time goes in v7:
time: 30.4 us; the launch traced here: 30.3 us
  Pallas kernels  29.6 us (97%)
  local copies, waits for them, and re-layouts  0.67 us (2%)
    pallas_call x1, Pallas kernels, per_device(): pl.pallas_call(lambda *refs: kernel(counts, *refs), name='correct', out_s...  29.6 us
    unnamed x1, local copies, waits for them, and re-layouts  0.67 us

profile of v7, /device:TPU:6, one launch (start us, length us, event | category | flops | bytes accessed | tf_op | source)
XLA Modules:
  0.0 30.3 jit_solution(175116876514729019)
XLA Ops:
  0.0 29.6 %correct.1 = f32[1,5,32,256]{3,2,1,0:T(8,128)S(1)} custom-call(f32[1,5,32,256]{3,2,1,0:T(8,128)} %refs_0_.1, bf16[1,3,5,32,256]{4,3,2,1,0:T(8,128)(2,1)} %refs_1_.1), custom_call_target="tpu_custom_call" | custom-call | tf_op jit(solution)/shard_map/correct/pallas_call | solution.py:288
  29.6 0.7 %copy.4 = f32[1,5,32,256]{3,2,1,0:T(8,128)} copy(f32[1,5,32,256]{3,2,1,0:T(8,128)S(1)} %correct.1) | data formatting | bytes 327680

commit v8 on v6

--- a/solution.py
+++ b/solution.py
@@ -142,6 +142,13 @@
     copies, up_copies = [], ()
     for tick in range(TICKS):
         now = u.at[tick]
+        to_x = (
+            remote(now.at[:, 0:8], x_hi.at[tick], x_ss.at[tick, 0], x_rs.at[tick, 0], {"gx": gx_down}),
+            remote(now.at[:, 24:32], x_lo.at[tick], x_ss.at[tick, 1], x_rs.at[tick, 1], {"gx": gx_up}),
+        )
+        if tick > 0:
+            for copy in to_x:
+                copy.start()
         for f in range(5):
             first, last = now[f, :, 0:128], now[f, :, 128:256]
             y_send[tick, 0, f] = jnp.where(
@@ -158,10 +165,6 @@
             remote(y_send.at[tick, 0], y_hi.at[tick], y_ss.at[tick, 0], y_rs.at[tick, 0], {"gy": gy_down}),
             remote(y_send.at[tick, 1], y_lo.at[tick], y_ss.at[tick, 1], y_rs.at[tick, 1], {"gy": gy_up}),
         )
-        to_x = (
-            remote(now.at[:, 0:8], x_hi.at[tick], x_ss.at[tick, 0], x_rs.at[tick, 0], {"gx": gx_down}),
-            remote(now.at[:, 24:32], x_lo.at[tick], x_ss.at[tick, 1], x_rs.at[tick, 1], {"gx": gx_up}),
-        )
         diagonal = (
             remote(y_send.at[tick, 0], d_hi.at[tick], d_ss.at[tick, 0], d_rs.at[tick, 0], {"sec": sec_up, "gy": gy_down}),
             remote(y_send.at[tick, 1], d_lo.at[tick], d_ss.at[tick, 1], d_rs.at[tick, 1], {"sec": sec_up, "gy": gy_up}),
@@ -181,7 +184,7 @@
             for copy in diagonal:
                 copy.start()
 
-        for copy in to_y + to_x:
+        for copy in to_y + (to_x if tick == 0 else ()):
             copy.start()
 
         copies += to_y + to_x

time: 29.5 us -> 29.5 us (level)
  no operation moved by 1% of the time
where the time goes in v8:
time: 29.5 us; the launch traced here: 29.3 us
  Pallas kernels  28.6 us (97%)
  local copies, waits for them, and re-layouts  0.67 us (2%)
    pallas_call x1, Pallas kernels, per_device(): pl.pallas_call(lambda *refs: kernel(counts, *refs), name='correct', out_s...  28.6 us
    unnamed x1, local copies, waits for them, and re-layouts  0.67 us

profile of v8, /device:TPU:6, one launch (start us, length us, event | category | flops | bytes accessed | tf_op | source)
XLA Modules:
  0.0 29.3 jit_solution(1351250197499288844)
XLA Ops:
  0.0 28.6 %correct.1 = f32[1,5,32,256]{3,2,1,0:T(8,128)S(1)} custom-call(f32[1,5,32,256]{3,2,1,0:T(8,128)} %refs_0_.1, bf16[1,3,5,32,256]{4,3,2,1,0:T(8,128)(2,1)} %refs_1_.1), custom_call_target="tpu_custom_call" | custom-call | tf_op jit(solution)/shard_map/correct/pallas_call | solution.py:292
  28.7 0.7 %copy.4 = f32[1,5,32,256]{3,2,1,0:T(8,128)} copy(f32[1,5,32,256]{3,2,1,0:T(8,128)S(1)} %correct.1) | data formatting | bytes 327680
